TPU v7x, 32 devices: a whole 2x2x4 slice. The times are simulated.
32 devices in a mesh: dp: 8 (over z, x), tensor: 4 (over y, core).
Axes of the slice: x: 2, y: 2, z: 4, core: 2. Of those that a mesh axis runs over, the one named last changes fastest.
Arguments:
- tokens: bfloat16 [8192, 1024], P(('dp', 'tensor')), may hold values from -6 to 6
- segments: int32 [8, 1024], P('dp'), may hold values from 0 to 11, never falling along the last dimension, each value on 1 to 512 neighbouring positions
- ln1_gain: float32 [1024], replicated, may hold values from 0.1 to 1.9
- ln1_bias: float32 [1024], replicated, may hold values from -1.75 to 1.75
- w_query: bfloat16 [1024, 1024], P('dp', 'tensor'), may hold values from -0.25 to 0.25
- b_query: float32 [1024], replicated, may hold values from -3 to 3
- w_key: bfloat16 [1024, 1024], P('dp', 'tensor'), may hold values from -0.25 to 0.25
- w_value: bfloat16 [1024, 1024], P('dp', 'tensor'), may hold values from -0.1875 to 0.1875
- b_value: float32 [1024], replicated, may hold values from -3 to 3
- head_scale: float32 [16], replicated, may hold values from 0.5 to 2
- w_out: bfloat16 [1024, 1024], P('tensor', 'dp'), may hold values from -0.1875 to 0.1875
- b_out: float32 [1024], replicated, may hold values from -3 to 3
- post_gain: float32 [1024], replicated, may hold values from 0.1 to 1.9
- post_bias: float32 [1024], replicated, may hold values from -1.75 to 1.75
- ln2_gain: float32 [1024], replicated, may hold values from 0.1 to 1.9
- ln2_bias: float32 [1024], replicated, may hold values from -1.75 to 1.75
- w_up: bfloat16 [1024, 4096], P('dp', 'tensor'), may hold values from -0.1875 to 0.1875
- b_up: float32 [4096], replicated, may hold values from -3 to 3
- ffn_gain: float32 [4096], replicated, may hold values from 0.1 to 1.9
- ffn_bias: float32 [4096], replicated, may hold values from -1.75 to 1.75
- w_down: bfloat16 [4096, 1024], P('tensor', 'dp'), may hold values from -0.09375 to 0.09375
- b_down: float32 [1024], replicated, may hold values from -1.75 to 1.75
- cotangent: bfloat16 [8192, 1024], P(('dp', 'tensor')), may hold values from -6 to 6
Outputs:
- output: bfloat16 [8192, 1024], P(('dp', 'tensor'))
- input_grad: float32 [8192, 1024], P(('dp', 'tensor'))
- grad_ln1_gain: float32 [1024], replicated
- grad_ln1_bias: float32 [1024], replicated
- grad_w_query: float32 [1024, 1024], P('dp', 'tensor')
- grad_b_query: float32 [1024], replicated
- grad_w_key: float32 [1024, 1024], P('dp', 'tensor')
- grad_w_value: float32 [1024, 1024], P('dp', 'tensor')
- grad_b_value: float32 [1024], replicated
- grad_head_scale: float32 [16], replicated
- grad_w_out: float32 [1024, 1024], P('tensor', 'dp')
- grad_b_out: float32 [1024], replicated
- grad_post_gain: float32 [1024], replicated
- grad_post_bias: float32 [1024], replicated
- grad_ln2_gain: float32 [1024], replicated
- grad_ln2_bias: float32 [1024], replicated
- grad_w_up: float32 [1024, 4096], P('dp', 'tensor')
- grad_b_up: float32 [4096], replicated
- grad_ffn_gain: float32 [4096], replicated
- grad_ffn_bias: float32 [4096], replicated
- grad_w_down: float32 [4096, 1024], P('tensor', 'dp')
- grad_b_down: float32 [1024], replicated
Inputs may be any that keep to these rules, and one draw needn't show every extreme that they name: `segments`: along each sequence segment numbers never fall; a document covers at most 512 positions, and some document covers exactly that many.
All inputs are finite; a program needn't handle non-finite values.
Results may differ from a plain program's by a relative error of at most 0.013.
The roundings to bfloat16 on the way count: a program that leaves them out, or rounds other values in their place, can miss the bound.
Values may be sent and summed in bfloat16 or wider, within the bound.
No kernel may reach another device: no remote copies, remote signals or barrier semaphores. Data moves between devices by JAX's collectives and lax.ppermute only.
A program may use at most 128 MiB of HBM per device.

v0:
```python
import jax
import jax.numpy as jnp
from jax import lax
from jax.sharding import PartitionSpec as P

D = 1024
HEADS = 16
HD = 64
FF = 4096


EPS = 1e-05


def norm_forward(values, gain, shift):
    mean = jnp.mean(values, axis=-1, keepdims=True)
    centered = values - mean
    inverse_scale = lax.rsqrt(jnp.mean(centered * centered, axis=-1, keepdims=True) + EPS)
    unit = centered * inverse_scale
    return (unit * gain + shift, unit, inverse_scale)


def norm_backward(grad, unit, inverse_scale, gain):
    scaled = grad * gain
    inner = (
        scaled
        - jnp.mean(scaled, axis=-1, keepdims=True)
        - unit * jnp.mean(scaled * unit, axis=-1, keepdims=True)
    )
    return (inverse_scale * inner, jnp.sum(grad * unit, axis=0), jnp.sum(grad, axis=0))


def gelu_slope(values):
    normal_cdf = 0.5 * (1.0 + lax.erf(values * 0.7071067811865476))
    density = jnp.exp(-0.5 * values * values) * 0.3989422804014327
    return normal_cdf + values * density


def contract_rows(left, right):
    return lax.dot_general(
        left, right, (((0,), (0,)), ((), ())), preferred_element_type=jnp.float32
    )


def contract_cols(left, right):
    return lax.dot_general(
        left, right, (((1,), (1,)), ((), ())), preferred_element_type=jnp.float32
    )


def own_part(vector, index, width_here):
    return lax.dynamic_slice_in_dim(vector, index * width_here, width_here, 0)


def place_part(vector, index, whole):
    return lax.dynamic_update_slice_in_dim(
        jnp.zeros((whole,), jnp.float32), vector, index * vector.shape[0], 0
    )


def row_totals(parts):
    return lax.psum(parts, "tensor")


def block_mask(segment, start, block):
    positions = jnp.arange(segment.shape[0], dtype=jnp.int32)
    row_pos = start + jnp.arange(block, dtype=jnp.int32)
    row_seg = lax.dynamic_slice_in_dim(segment, start, block, 0)
    return (positions[None, :] <= row_pos[:, None]) & (segment[None, :] == row_seg[:, None])


def attend_forward(query, keys, values, segment, block, scale):
    length, heads_here, head_size = query.shape

    def one_block(start):
        rows_q = lax.dynamic_slice_in_dim(query, start, block, 0)
        allowed = block_mask(segment, start, block)
        raw = jnp.einsum("qhd,khd->hqk", rows_q, keys, preferred_element_type=jnp.float32)
        scores = jnp.where(allowed[None], raw * scale, -1000000000.0)
        highest = jnp.max(scores, axis=-1, keepdims=True)
        lse = jnp.log(jnp.sum(jnp.exp(scores - highest), axis=-1, keepdims=True)) + highest
        probs = jnp.exp(scores - lse).astype(jnp.bfloat16)
        mixed = jnp.einsum("hqk,khd->qhd", probs, values, preferred_element_type=jnp.float32)
        return (mixed, lse[..., 0])

    starts = jnp.arange(0, length, block, dtype=jnp.int32)
    mixed, totals = lax.map(one_block, starts)
    return (mixed.reshape(length, heads_here, head_size), totals)


def attend_backward(query, keys, values, segment, totals, grad_mixed, block, scale):
    length, heads_here, head_size = query.shape

    def one_block(carry, item):
        grad_keys, grad_values = carry
        start, lse = item
        rows_q = lax.dynamic_slice_in_dim(query, start, block, 0)
        grad_rows = lax.dynamic_slice_in_dim(grad_mixed, start, block, 0)
        allowed = block_mask(segment, start, block)
        raw = jnp.einsum("qhd,khd->hqk", rows_q, keys, preferred_element_type=jnp.float32)
        scores = jnp.where(allowed[None], raw * scale, -1000000000.0)
        probs = jnp.exp(scores - lse[..., None])
        rounded = probs.astype(jnp.bfloat16)
        grad_values = grad_values + jnp.einsum(
            "hqk,qhd->khd", rounded, grad_rows, preferred_element_type=jnp.float32
        )
        grad_probs = jnp.einsum(
            "qhd,khd->hqk", grad_rows, values, preferred_element_type=jnp.float32
        )
        delta = jnp.sum(probs * grad_probs, axis=-1, keepdims=True)
        grad_raw = (probs * (grad_probs - delta) * scale).astype(jnp.bfloat16)
        grad_query_rows = jnp.einsum(
            "hqk,khd->qhd", grad_raw, keys, preferred_element_type=jnp.float32
        )
        grad_keys = grad_keys + jnp.einsum(
            "hqk,qhd->khd", grad_raw, rows_q, preferred_element_type=jnp.float32
        )
        return ((grad_keys, grad_values), grad_query_rows)

    starts = jnp.arange(0, length, block, dtype=jnp.int32)
    zeros = jnp.zeros((length, heads_here, head_size), jnp.float32)
    (grad_keys, grad_values), grad_query = lax.scan(one_block, (zeros, zeros), (starts, totals))
    return (grad_query.reshape(length, heads_here, head_size), grad_keys, grad_values)


def per_device(
    tokens,
    segments,
    ln1_gain,
    ln1_bias,
    w_query,
    b_query,
    w_key,
    w_value,
    b_value,
    head_scale,
    w_out,
    b_out,
    post_gain,
    post_bias,
    ln2_gain,
    ln2_bias,
    w_up,
    b_up,
    ffn_gain,
    ffn_bias,
    w_down,
    b_down,
    cotangent,
):
    groups = lax.axis_size("tensor")
    index = lax.axis_index("tensor")
    local_rows = tokens.shape[0]
    length = local_rows * groups
    query_w, key_w, value_w, out_w, up_w, down_w = (
        lax.all_gather(w_query, "dp", axis=0, tiled=True),
        lax.all_gather(w_key, "dp", axis=0, tiled=True),
        lax.all_gather(w_value, "dp", axis=0, tiled=True),
        lax.all_gather(w_out, "dp", axis=1, tiled=True),
        lax.all_gather(w_up, "dp", axis=0, tiled=True),
        lax.all_gather(w_down, "dp", axis=1, tiled=True),
    )
    columns = query_w.shape[1]
    heads_here = columns // HD
    hidden_here = up_w.shape[1]
    segment = segments[0]
    block = min(512, length)
    scale = HD ** (-0.5)
    inputs = tokens.astype(jnp.float32)
    normed, unit_one, inverse_one = norm_forward(inputs, ln1_gain, ln1_bias)
    normed_all = lax.all_gather(normed.astype(jnp.bfloat16), "tensor", axis=0, tiled=True)
    query = (
        jnp.dot(normed_all, query_w, preferred_element_type=jnp.float32)
        + own_part(b_query, index, columns)
    ).astype(jnp.bfloat16)
    keys = jnp.dot(normed_all, key_w, preferred_element_type=jnp.float32).astype(jnp.bfloat16)
    values = (
        jnp.dot(normed_all, value_w, preferred_element_type=jnp.float32)
        + own_part(b_value, index, columns)
    ).astype(jnp.bfloat16)
    query_heads = query.reshape(length, heads_here, HD)
    key_heads = keys.reshape(length, heads_here, HD)
    value_heads = values.reshape(length, heads_here, HD)
    mixed, totals = attend_forward(query_heads, key_heads, value_heads, segment, block, scale)
    scales_here = own_part(head_scale, index, heads_here)
    scaled = (mixed * scales_here[None, :, None]).reshape(length, columns).astype(jnp.bfloat16)
    projected = (
        lax.psum_scatter(
            jnp.dot(scaled, out_w, preferred_element_type=jnp.float32),
            "tensor",
            scatter_dimension=0,
            tiled=True,
        )
        + b_out
    )
    post, unit_two, inverse_two = norm_forward(projected, post_gain, post_bias)
    hidden = inputs + post
    ffn_in, unit_three, inverse_three = norm_forward(hidden, ln2_gain, ln2_bias)
    ffn_all = lax.all_gather(ffn_in.astype(jnp.bfloat16), "tensor", axis=0, tiled=True)
    before_gelu = jnp.dot(ffn_all, up_w, preferred_element_type=jnp.float32) + own_part(
        b_up, index, hidden_here
    )
    active = jax.nn.gelu(before_gelu, approximate=False)
    mean = row_totals(jnp.sum(active, axis=-1)) / FF
    centered = active - mean[:, None]
    variance = row_totals(jnp.sum(centered * centered, axis=-1)) / FF
    inverse_four = lax.rsqrt(variance + EPS)[:, None]
    unit_four = centered * inverse_four
    gain_here = own_part(ffn_gain, index, hidden_here)
    inner = (unit_four * gain_here + own_part(ffn_bias, index, hidden_here)).astype(jnp.bfloat16)
    branch = (
        lax.psum_scatter(
            jnp.dot(inner, down_w, preferred_element_type=jnp.float32),
            "tensor",
            scatter_dimension=0,
            tiled=True,
        )
        + b_down
    )
    output = (hidden + branch).astype(jnp.bfloat16)
    grad_out = cotangent.astype(jnp.float32)
    grad_all = lax.all_gather(cotangent, "tensor", axis=0, tiled=True)
    grad_down = contract_rows(inner, grad_all)
    grad_inner = contract_cols(grad_all, down_w)
    grad_gain_here = jnp.sum(grad_inner * unit_four, axis=0)
    grad_shift_here = jnp.sum(grad_inner, axis=0)
    scaled_grad = grad_inner * gain_here
    total_plain, total_unit = lax.psum(
        (jnp.sum(scaled_grad, axis=-1), jnp.sum(scaled_grad * unit_four, axis=-1)), "tensor"
    )
    grad_active = inverse_four * (
        scaled_grad - total_plain[:, None] / FF - unit_four * total_unit[:, None] / FF
    )
    grad_before = (grad_active * gelu_slope(before_gelu)).astype(jnp.bfloat16)
    grad_b_up_here = jnp.sum(grad_before.astype(jnp.float32), axis=0)
    grad_up = contract_rows(ffn_all, grad_before)
    grad_ffn_in = lax.psum_scatter(
        contract_cols(grad_before, up_w), "tensor", scatter_dimension=0, tiled=True
    )
    grad_norm_two, grad_ln2_gain, grad_ln2_bias = norm_backward(
        grad_ffn_in, unit_three, inverse_three, ln2_gain
    )
    grad_hidden = grad_out + grad_norm_two
    grad_proj, grad_post_gain, grad_post_bias = norm_backward(
        grad_hidden, unit_two, inverse_two, post_gain
    )
    grad_proj_low = grad_proj.astype(jnp.bfloat16)
    grad_b_out = jnp.sum(grad_proj_low.astype(jnp.float32), axis=0)
    grad_proj_all = lax.all_gather(grad_proj_low, "tensor", axis=0, tiled=True)
    grad_out_w = contract_rows(scaled, grad_proj_all)
    grad_scaled = contract_cols(grad_proj_all, out_w).reshape(length, heads_here, HD)
    grad_scales_here = jnp.sum(grad_scaled * mixed, axis=(0, 2))
    grad_mixed = (grad_scaled * scales_here[None, :, None]).astype(jnp.bfloat16)
    grad_query, grad_keys, grad_values = attend_backward(
        query_heads, key_heads, value_heads, segment, totals, grad_mixed, block, scale
    )
    grad_query = grad_query.reshape(length, columns).astype(jnp.bfloat16)
    grad_keys = grad_keys.reshape(length, columns).astype(jnp.bfloat16)
    grad_values = grad_values.reshape(length, columns).astype(jnp.bfloat16)
    grad_b_query_here = jnp.sum(grad_query.astype(jnp.float32), axis=0)
    grad_b_value_here = jnp.sum(grad_values.astype(jnp.float32), axis=0)
    grad_query_w = contract_rows(normed_all, grad_query)
    grad_key_w = contract_rows(normed_all, grad_keys)
    grad_value_w = contract_rows(normed_all, grad_values)
    grad_normed = lax.psum_scatter(
        contract_cols(grad_query, query_w)
        + contract_cols(grad_keys, key_w)
        + contract_cols(grad_values, value_w),
        "tensor",
        scatter_dimension=0,
        tiled=True,
    )
    grad_norm_one, grad_ln1_gain, grad_ln1_bias = norm_backward(
        grad_normed, unit_one, inverse_one, ln1_gain
    )
    input_grad = grad_hidden + grad_norm_one
    grad_b_down = jnp.sum(grad_out, axis=0)
    g_query_w, g_key_w, g_value_w, g_out_w, g_up_w, g_down_w = (
        lax.psum_scatter(grad_query_w, "dp", scatter_dimension=0, tiled=True),
        lax.psum_scatter(grad_key_w, "dp", scatter_dimension=0, tiled=True),
        lax.psum_scatter(grad_value_w, "dp", scatter_dimension=0, tiled=True),
        lax.psum_scatter(grad_out_w, "dp", scatter_dimension=1, tiled=True),
        lax.psum_scatter(grad_up, "dp", scatter_dimension=0, tiled=True),
        lax.psum_scatter(grad_down, "dp", scatter_dimension=1, tiled=True),
    )
    (
        s_ln1_gain,
        s_ln1_bias,
        s_b_query,
        s_b_value,
        s_head_scale,
        s_b_out,
        s_post_gain,
        s_post_bias,
        s_ln2_gain,
        s_ln2_bias,
        s_b_up,
        s_ffn_gain,
        s_ffn_bias,
        s_b_down,
    ) = lax.psum(
        (
            grad_ln1_gain,
            grad_ln1_bias,
            place_part(grad_b_query_here, index, D),
            place_part(grad_b_value_here, index, D),
            place_part(grad_scales_here, index, HEADS),
            grad_b_out,
            grad_post_gain,
            grad_post_bias,
            grad_ln2_gain,
            grad_ln2_bias,
            place_part(grad_b_up_here, index, FF),
            place_part(grad_gain_here, index, FF),
            place_part(grad_shift_here, index, FF),
            grad_b_down,
        ),
        ("dp", "tensor"),
    )
    return (
        output,
        input_grad,
        s_ln1_gain,
        s_ln1_bias,
        g_query_w,
        s_b_query,
        g_key_w,
        g_value_w,
        s_b_value,
        s_head_scale,
        g_out_w,
        s_b_out,
        s_post_gain,
        s_post_bias,
        s_ln2_gain,
        s_ln2_bias,
        g_up_w,
        s_b_up,
        s_ffn_gain,
        s_ffn_bias,
        g_down_w,
        s_b_down,
    )


def solution(mesh):
    return jax.shard_map(
        per_device,
        mesh=mesh,
        in_specs=(
            P(("dp", "tensor"), None),
            P("dp", None),
            P(),
            P(),
            P("dp", "tensor"),
            P(),
            P("dp", "tensor"),
            P("dp", "tensor"),
            P(),
            P(),
            P("tensor", "dp"),
            P(),
            P(),
            P(),
            P(),
            P(),
            P("dp", "tensor"),
            P(),
            P(),
            P(),
            P("tensor", "dp"),
            P(),
            P(("dp", "tensor"), None),
        ),
        out_specs=(
            P(("dp", "tensor"), None),
            P(("dp", "tensor"), None),
            P(),
            P(),
            P("dp", "tensor"),
            P(),
            P("dp", "tensor"),
            P("dp", "tensor"),
            P(),
            P(),
            P("tensor", "dp"),
            P(),
            P(),
            P(),
            P(),
            P(),
            P("dp", "tensor"),
            P(),
            P(),
            P(),
            P("tensor", "dp"),
            P(),
        ),
        check_vma=False,
    )
```

profile of v0, /device:TPU:0, one launch (start us, length us, event | category | flops | bytes accessed | tf_op | source)
XLA Modules:
  0.0 1348.6 jit_solution(8178695233809237348)
XLA Ops:
  15.0 33.3 %all_gather.31 = bf16[1024,256]{1,0:T(8,128)(2,1)S(1)} all-gather(bf16[128,256]{1,0:T(8,128)(2,1)} %param.31), channel_id=1, replica_groups=mesh['dp'=8,'tensor'=4] {'dp'}, dimensions={0}, use_global_device_ids=true | all-gather | bytes 589824 | tf_op jit(solution)/shard_map/all_gather | solution.py:156
  48.4 31.6 %all_gather.32 = bf16[1024,256]{1,0:T(8,128)(2,1)S(1)} all-gather(bf16[128,256]{1,0:T(8,128)(2,1)} %param.33), channel_id=1, replica_groups=mesh['dp'=8,'tensor'=4] {'dp'}, dimensions={0}, use_global_device_ids=true | all-gather | bytes 589824 | tf_op jit(solution)/shard_map/all_gather | solution.py:157
  80.0 31.7 %all_gather.33 = bf16[1024,256]{1,0:T(8,128)(2,1)S(1)} all-gather(bf16[128,256]{1,0:T(8,128)(2,1)} %param.34), channel_id=1, replica_groups=mesh['dp'=8,'tensor'=4] {'dp'}, dimensions={0}, use_global_device_ids=true | all-gather | bytes 589824 | tf_op jit(solution)/shard_map/all_gather | solution.py:158
  111.7 27.0 %all_gather.34 = bf16[256,1024]{1,0:T(8,128)(2,1)S(1)} all-gather(bf16[256,128]{1,0:T(8,128)(2,1)S(1)} %copy-done.31), channel_id=1, replica_groups=mesh['dp'=8,'tensor'=4] {'dp'}, dimensions={1}, use_global_device_ids=true | all-gather | bytes 589824 | tf_op jit(solution)/shard_map/all_gather | solution.py:159
  144.5 42.6 %while.27 = (s32[]{:T(128)}, f32[2,512,4,64]{1,0,3,2:T(2,128)}, f32[2,4,512]{2,1,0:T(4,128)S(1)}, s32[2]{0:T(128)S(1)}, s32[1,1024]{1,0:T(1,128)S(1)}, /*index=5...) while((s32[]{:T(128)}, f32[2,512,4,64]{1,0,3,2:T(2,128)}, ...), condition=%wide.region_5.6_spmd, body=%wide.region_2.5_spmd.sunk | while | flops 561510912 | bytes 31275200 | solution.py:87
  155.4 10.4 dynamic_update_slice.42
  176.7 10.4 dynamic_update_slice.42
  194.7 42.2 %reduce-scatter.11.cloned.1.call-done = f32[256,1024]{1,0:T(8,128)} async-done(((f32[1024,1024]{1,0:T(8,128)}), f32[256,1024]{1,0:T(8,128)}) %reduce-scatter.11.cloned.1.call-update) | async-done | bytes 1048592 | tf_op jit(solution)/shard_map/reduce_scatter | solution.py:188
  244.5 16.6 %all-gather.15.cloned.1.call-done = bf16[1024,1024]{1,0:T(8,128)(2,1)} async-done(((bf16[256,1024]{1,0:T(8,128)(2,1)}), bf16[1024,1024]{1,0:T(8,128)(2,1)}) %all-gather.15.cloned.1.call-update) | async-done | bytes 2097168 | tf_op jit(solution)/shard_map/all_gather | solution.py:222
  261.1 52.3 %all-gather.13.cloned.1.call-done = bf16[1024,1024]{1,0:T(8,128)(2,1)} async-done(((bf16[1024,128]{1,0:T(8,128)(2,1)}), bf16[1024,1024]{1,0:T(8,128)(2,1)}) %all-gather.13.cloned.1.call-update) | async-done | bytes 2097168 | tf_op jit(solution)/shard_map/all_gather | solution.py:161
  313.4 7.2 fusion.120
  320.5 5.4 copy.53
  326.0 36.7 %all-gather.11.cloned.1.call-done = bf16[1024,1024]{1,0:T(8,128)(2,1)} async-done(((bf16[128,1024]{1,0:T(8,128)(2,1)}), bf16[1024,1024]{1,0:T(8,128)(2,1)}) %all-gather.11.cloned.1.call-update) | async-done | bytes 2097168 | tf_op jit(solution)/shard_map/all_gather | solution.py:160
  362.7 23.1 %all-gather.9.cloned.1.call-done = bf16[1024,1024]{1,0:T(8,128)(2,1)} async-done(((bf16[256,1024]{1,0:T(8,128)(2,1)}), bf16[1024,1024]{1,0:T(8,128)(2,1)}) %all-gather.9.cloned.1.call-update) | async-done | bytes 2097168 | tf_op jit(solution)/shard_map/all_gather | solution.py:199
  385.8 15.1 %fusion.117 = (f32[1024]{0:T(1024)S(1)}, f32[1024,1024]{0,1:T(8,128)}, f32[1024,1024]{0,1:T(8,128)}) fusion(f32[1024]{0:T(1024)S(1)} %dynamic_slice.47, bf16[1024,1024]{1,0:T(8,128)(2,1)} %all-gather.9.cloned.1.call-done, bf16[1024,1024]{1,0:T(8,128)(2,1)} %all-gather.11.cloned.1.call-done), kind=kOutput, calls=%fused_computation.161 | convolution fusion | flops 2216688640 | bytes 12591104 | tf_op jit(solution)/shard_map/dot_general | solution.py:200
  400.9 5.9 psum.126
  409.4 5.7 psum.127
  415.1 4.3 multiply_reduce_fusion.1
  419.4 7.6 all-reduce.1
  427.0 6.8 convert_reduce_fusion
  435.1 4.3 fusion.121
  440.2 7.5 fusion.115
  447.7 36.4 %reduce-scatter.15.cloned.1.call-done = f32[256,1024]{1,0:T(8,128)} async-done(((f32[1024,1024]{1,0:T(8,128)}), f32[256,1024]{1,0:T(8,128)}) %reduce-scatter.15.cloned.1.call-update) | async-done | bytes 1048592 | tf_op jit(solution)/shard_map/reduce_scatter | solution.py:237
  486.5 44.8 %reduce-scatter.13.cloned.1.call-done = f32[256,1024]{1,0:T(8,128)} async-done(((f32[1024,1024]{1,0:T(8,128)}), f32[256,1024]{1,0:T(8,128)}) %reduce-scatter.13.cloned.1.call-update) | async-done | bytes 1048592 | tf_op jit(solution)/shard_map/reduce_scatter | solution.py:212
  531.3 4.1 multiply_reduce_fusion.6
  537.3 22.6 %all-gather.17.cloned.1.call-done = bf16[1024,1024]{1,0:T(8,128)(2,1)} async-done(((bf16[256,1024]{1,0:T(8,128)(2,1)}), bf16[1024,1024]{1,0:T(8,128)(2,1)}) %all-gather.17.cloned.1.call-update) | async-done | bytes 2097168 | tf_op jit(solution)/shard_map/all_gather | solution.py:249
  563.4 110.5 %while.28 = (s32[]{:T(128)}, f32[1024,4,64]{0,2,1:T(8,128)}, f32[1024,4,64]{0,2,1:T(8,128)}, bf16[2,512,4,64]{1,3,2,0:T(8,128)(2,1)}, s32[2]{0:T(128)S(1)}, /*in...) while((s32[]{:T(128)}, f32[1024,4,64]{0,2,1:T(8,128)}, ...), condition=%wide.region_27.28_spmd.clone, body=%wide.region_25.27_spmd.clone.sunk | while | flops 1399331328 | bytes 138484016 | solution.py:122
  568.8 3.6 fusion.205
  572.4 4.6 fusion.201
  577.0 17.8 %fusion.206 = bf16[2,512,4,64]{1,3,2,0:T(8,128)(2,1)} fusion(bf16[2,512,4,64]{1,3,2,0:T(8,128)(2,1)} %get-tuple-element.465, s32[]{:T(128)S(6)} %copy.109, bf16[1024,4,64]{0,2,1:T(8,128)(2,1)S(1)} %get-tuple-element.485, f32[4,512,1024]{2,1,0:T(8,128)} %fusion.201, f32[4,512,1024]{2,1,0:T(8,128)} %copy-done, ...), kind=kOutput, calls=%fused_computation.42.clone.1 | convolution fusion | flops 291507200 | bytes 35667972 | tf_op jit(solution)/shard_map/while/body/eval_jaxpr/hqk,khd->qhd/dot_general | solution.py:112
  594.8 23.1 %fusion.204 = f32[1024,4,64]{0,2,1:T(8,128)} fusion(f32[4,512,1024]{2,1,0:T(8,128)} %fusion.201, f32[4,512,1024]{2,1,0:T(8,128)} %copy-done, f32[4,512]{1,0:T(4,128)S(1)} %dynamic-slice_bitcast_fusion.2, pred[512,1024]{1,0:T(8,128)(4,1)S(1)} %fusion.203, f32[1024,4,64]{0,2,1:T(8,128)} %get-tuple-element.463, pred[]{:T(512)S(6)} %compare.3, ...), kind=kOutput, calls=%fused_computation.39.clone.1 | convolution fusion | flops 292031488 | bytes 36978692 | tf_op jit(solution)/shard_map/while/body/eval_jaxpr/hqk,qhd->khd/dot_general | solution.py:115
  623.1 5.0 fusion.205
  628.2 4.6 fusion.201
  632.8 17.8 %fusion.206 = bf16[2,512,4,64]{1,3,2,0:T(8,128)(2,1)} fusion(bf16[2,512,4,64]{1,3,2,0:T(8,128)(2,1)} %get-tuple-element.465, s32[]{:T(128)S(6)} %copy.109, bf16[1024,4,64]{0,2,1:T(8,128)(2,1)S(1)} %get-tuple-element.485, f32[4,512,1024]{2,1,0:T(8,128)} %fusion.201, f32[4,512,1024]{2,1,0:T(8,128)} %copy-done, ...), kind=kOutput, calls=%fused_computation.42.clone.1 | convolution fusion | flops 291507200 | bytes 35667972 | tf_op jit(solution)/shard_map/while/body/eval_jaxpr/hqk,khd->qhd/dot_general | solution.py:112
  650.6 23.2 %fusion.204 = f32[1024,4,64]{0,2,1:T(8,128)} fusion(f32[4,512,1024]{2,1,0:T(8,128)} %fusion.201, f32[4,512,1024]{2,1,0:T(8,128)} %copy-done, f32[4,512]{1,0:T(4,128)S(1)} %dynamic-slice_bitcast_fusion.2, pred[512,1024]{1,0:T(8,128)(4,1)S(1)} %fusion.203, f32[1024,4,64]{0,2,1:T(8,128)} %get-tuple-element.463, pred[]{:T(512)S(6)} %compare.3, ...), kind=kOutput, calls=%fused_computation.39.clone.1 | convolution fusion | flops 292031488 | bytes 36978692 | tf_op jit(solution)/shard_map/while/body/eval_jaxpr/hqk,qhd->khd/dot_general | solution.py:115
  684.8 5.9 fusion.127
  692.8 6.8 fusion.114
  700.3 3.4 fusion.112
  703.8 2.8 fusion.126
  713.9 14.1 %reduce-scatter.17.cloned.1.call-done = f32[256,1024]{1,0:T(8,128)} async-done(((f32[1024,1024]{1,0:T(8,128)}), f32[256,1024]{1,0:T(8,128)}) %reduce-scatter.17.cloned.1.call-update) | async-done | bytes 1048592 | tf_op jit(solution)/shard_map/reduce_scatter | solution.py:265
  730.4 2.9 fusion.109
  733.3 87.3 %reduce-scatter.27.cloned.1.call-done = f32[128,1024]{1,0:T(8,128)} async-done(((f32[1024,1024]{1,0:T(8,128)}), f32[128,1024]{1,0:T(8,128)}) %reduce-scatter.27.cloned.1.call-update) | async-done | bytes 524304 | tf_op jit(solution)/shard_map/reduce_scatter | solution.py:283
  820.6 92.4 %reduce-scatter.29.cloned.1.call-done = f32[1024,128]{1,0:T(8,128)} async-done(((f32[1024,1024]{1,0:T(8,128)}), f32[1024,128]{1,0:T(8,128)}) %reduce-scatter.29.cloned.1.call-update) | async-done | bytes 524304 | tf_op jit(solution)/shard_map/reduce_scatter | solution.py:284
  913.0 68.2 %reduce-scatter.25.cloned.1.call-done = f32[256,128]{1,0:T(8,128)} async-done(((f32[256,1024]{1,0:T(8,128)}), f32[256,128]{1,0:T(8,128)}) %reduce-scatter.25.cloned.1.call-update) | async-done | bytes 131088 | tf_op jit(solution)/shard_map/reduce_scatter | solution.py:282
  981.2 66.9 %reduce-scatter.23.cloned.1.call-done = f32[128,256]{1,0:T(8,128)} async-done(((f32[1024,256]{1,0:T(8,128)}), f32[128,256]{1,0:T(8,128)}) %reduce-scatter.23.cloned.1.call-update) | async-done | bytes 131088 | tf_op jit(solution)/shard_map/reduce_scatter | solution.py:281
  1048.1 67.0 %reduce-scatter.21.cloned.1.call-done = f32[128,256]{1,0:T(8,128)} async-done(((f32[1024,256]{1,0:T(8,128)}), f32[128,256]{1,0:T(8,128)}) %reduce-scatter.21.cloned.1.call-update) | async-done | bytes 131088 | tf_op jit(solution)/shard_map/reduce_scatter | solution.py:280
  1115.1 67.0 %reduce-scatter.19.cloned.1.call-done = f32[128,256]{1,0:T(8,128)} async-done(((f32[1024,256]{1,0:T(8,128)}), f32[128,256]{1,0:T(8,128)}) %reduce-scatter.19.cloned.1.call-update) | async-done | bytes 131088 | tf_op jit(solution)/shard_map/reduce_scatter | solution.py:279
  1182.1 141.7 %all-reduce.4.cloned.1.call-done = (f32[1024]{0:T(1024)}, f32[1024]{0:T(1024)}, f32[1024]{0:T(1024)}, f32[1024]{0:T(1024)}, f32[16]{0:T(128)}, /*index=5*/f32[10...) async-done(((f32[1024]{0:T(1024)}, f32[1024]{0:T(1024)}, ...) | async-done | bytes 90192 | tf_op jit(solution)/shard_map/psum | solution.py:301
  (262 shorter events, 106.1 us)
Async XLA Ops:
  7.2 104.5 %copy-start.31 = (bf16[256,128]{1,0:T(8,128)(2,1)S(1)}, bf16[256,128]{1,0:T(8,128)(2,1)}, u32[]{:S(2)}) copy-start(bf16[256,128]{1,0:T(8,128)(2,1)} %param.37) | copy-start | bytes 196612
  7.2 131.5 %all-gather.7.cloned.1.call-start = ((), (), s32[]{:S(2)}) async-start(), calls=%async_computation.10 | async-start | bytes 2621440 | tf_op jit(solution)/shard_map/all_gather | solution.py:171
  12.5 224.4 %reduce-scatter.11.cloned.1.call-start = ((), (), s32[]{:S(2)}) async-start(), calls=%async_computation.11 | async-start | bytes 5242880 | tf_op jit(solution)/shard_map/reduce_scatter | solution.py:188
  15.0 173.9 %copy-start.36 = (f32[256]{0:T(256)}, f32[256]{0:T(256)S(1)}, u32[]{:S(2)}) copy-start(f32[256]{0:T(256)S(1)} %mul.289) | copy-start | bytes 3076
  48.3 95.3 %copy-start.20 = (bf16[1024,256]{1,0:T(8,128)(2,1)}, bf16[1024,256]{1,0:T(8,128)(2,1)S(1)}, u32[]{:S(2)}) copy-start(bf16[1024,256]{1,0:T(8,128)(2,1)S(1)} %all_gather.31) | copy-start | bytes 1572868
  80.0 58.7 %copy-start.22 = (bf16[1024,256]{1,0:T(8,128)(2,1)}, bf16[1024,256]{1,0:T(8,128)(2,1)S(1)}, u32[]{:S(2)}) copy-start(bf16[1024,256]{1,0:T(8,128)(2,1)S(1)} %all_gather.32) | copy-start | bytes 1572868
  111.6 29.6 %copy-start.27 = (bf16[1024,256]{1,0:T(8,128)(2,1)}, bf16[1024,256]{1,0:T(8,128)(2,1)S(1)}, u32[]{:S(2)}) copy-start(bf16[1024,256]{1,0:T(8,128)(2,1)S(1)} %all_gather.33) | copy-start | bytes 1572868
  138.7 50.2 %copy-start.16 = (bf16[256,1024]{1,0:T(8,128)(2,1)}, bf16[256,1024]{1,0:T(8,128)(2,1)S(1)}, u32[]{:S(2)}) copy-start(bf16[256,1024]{1,0:T(8,128)(2,1)S(1)} %all_gather.34) | copy-start | bytes 1572868
  187.1 5.7 copy-start.8
  187.1 5.7 copy-start.10
  190.0 47.0 %copy-start.30 = (f32[1024]{0:T(1024)S(1)}, f32[1024]{0:T(1024)}, u32[]{:S(2)}) copy-start(f32[1024]{0:T(1024)} %param.38) | copy-start | bytes 12292
  192.7 47.1 %copy-start.6 = (bf16[256,1024]{1,0:T(8,128)(2,1)S(1)}, bf16[256,1024]{1,0:T(8,128)(2,1)}, u32[]{:S(2)}) copy-start(bf16[256,1024]{1,0:T(8,128)(2,1)} %param.27) | copy-start | bytes 1572868
  192.7 47.1 %copy-start.39 = (f32[1024]{0:T(1024)S(1)}, f32[1024]{0:T(1024)}, u32[]{:S(2)}) copy-start(f32[1024]{0:T(1024)} %param.39) | copy-start | bytes 12292
  192.7 47.1 %copy-start.46 = (f32[1024]{0:T(1024)S(1)}, f32[1024]{0:T(1024)}, u32[]{:S(2)}) copy-start(f32[1024]{0:T(1024)} %param.40) | copy-start | bytes 12292
  192.8 49.0 %copy-start.38 = (f32[1024]{0:T(1024)S(1)}, f32[1024]{0:T(1024)}, u32[]{:S(2)}) copy-start(f32[1024]{0:T(1024)} %param.41) | copy-start | bytes 12292
  192.8 49.0 %copy-start.47 = (f32[1024]{0:T(1024)S(1)}, f32[1024]{0:T(1024)}, u32[]{:S(2)}) copy-start(f32[1024]{0:T(1024)} %param.42) | copy-start | bytes 12292
  192.8 68.3 %all-gather.15.cloned.1.call-start = ((), (), s32[]{:S(2)}) async-start(), calls=%async_computation.16 | async-start | bytes 2621440 | tf_op jit(solution)/shard_map/all_gather | solution.py:222
  193.5 119.9 %all-gather.13.cloned.1.call-start = ((), (), s32[]{:S(2)}) async-start(), calls=%async_computation.14 | async-start | bytes 2359296 | tf_op jit(solution)/shard_map/all_gather | solution.py:161
  194.1 168.6 %all-gather.11.cloned.1.call-start = ((), (), s32[]{:S(2)}) async-start(), calls=%async_computation.13 | async-start | bytes 2359296 | tf_op jit(solution)/shard_map/all_gather | solution.py:160
  194.7 191.1 %all-gather.9.cloned.1.call-start = ((), (), s32[]{:S(2)}) async-start(), calls=%async_computation.12 | async-start | bytes 2621440 | tf_op jit(solution)/shard_map/all_gather | solution.py:199
  242.9 241.3 %reduce-scatter.15.cloned.1.call-start = ((), (), s32[]{:S(2)}) async-start(), calls=%async_computation.17 | async-start | bytes 5242880 | tf_op jit(solution)/shard_map/reduce_scatter | solution.py:237
  427.0 8.1 copy-start.52
  439.4 91.9 %reduce-scatter.13.cloned.1.call-start = ((), (), s32[]{:S(2)}) async-start(), calls=%async_computation.15 | async-start | bytes 5242880 | tf_op jit(solution)/shard_map/reduce_scatter | solution.py:212
  447.7 83.7 %copy-start.3 = (f32[256,1024]{1,0:T(8,128)S(1)}, f32[256,1024]{1,0:T(8,128)}, u32[]{:S(2)}) copy-start(f32[256,1024]{1,0:T(8,128)} %reduce-scatter.11.cloned.1.call-done) | copy-start | bytes 3145732
  447.7 83.7 %copy-start.26 = (bf16[256,1024]{1,0:T(8,128)(2,1)S(1)}, bf16[256,1024]{1,0:T(8,128)(2,1)}, u32[]{:S(2)}) copy-start(bf16[256,1024]{1,0:T(8,128)(2,1)} %param.49) | copy-start | bytes 1572868
  447.7 83.7 %copy-start.49 = (f32[1024]{0:T(1024)S(1)}, f32[1024]{0:T(1024)}, u32[]{:S(2)}) copy-start(f32[1024]{0:T(1024)} %param.48) | copy-start | bytes 12292
  447.7 112.3 %all-gather.17.cloned.1.call-start = ((), (), s32[]{:S(2)}) async-start(), calls=%async_computation.18 | async-start | bytes 2621440 | tf_op jit(solution)/shard_map/all_gather | solution.py:249
  535.4 24.6 %copy-start.5 = (f32[32,8,2,512]{3,1,2,0:T(8,128)S(1)}, f32[32,8,2,512]{3,1,2,0:T(8,128)}, u32[]{:S(2)}) copy-start(f32[32,8,2,512]{3,1,2,0:T(8,128)} %copy-done.4) | copy-start | bytes 3145732
  537.2 190.7 %reduce-scatter.17.cloned.1.call-start = ((), (), s32[]{:S(2)}) async-start(), calls=%async_computation.19 | async-start | bytes 5242880 | tf_op jit(solution)/shard_map/reduce_scatter | solution.py:265
  537.3 26.1 %copy-start.9 = (bf16[1024,4,64]{0,2,1:T(8,128)(2,1)S(1)}, bf16[1024,4,64]{0,2,1:T(8,128)(2,1)}, u32[]{:S(2)}) copy-start(bf16[1024,4,64]{0,2,1:T(8,128)(2,1)} %copy-done.8) | copy-start | bytes 1572868
  537.3 26.1 %copy-start.11 = (bf16[1024,4,64]{0,2,1:T(8,128)(2,1)S(1)}, bf16[1024,4,64]{0,2,1:T(8,128)(2,1)}, u32[]{:S(2)}) copy-start(bf16[1024,4,64]{0,2,1:T(8,128)(2,1)} %copy-done.10) | copy-start | bytes 1572868
  683.2 137.3 %reduce-scatter.27.cloned.1.call-start = ((), (), s32[]{:S(2)}) async-start(), calls=%async_computation.24 | async-start | bytes 4718592 | tf_op jit(solution)/shard_map/reduce_scatter | solution.py:283
  690.7 222.2 %reduce-scatter.29.cloned.1.call-start = ((), (), s32[]{:S(2)}) async-start(), calls=%async_computation.25 | async-start | bytes 4718592 | tf_op jit(solution)/shard_map/reduce_scatter | solution.py:284
  699.7 281.5 %reduce-scatter.25.cloned.1.call-start = ((), (), s32[]{:S(2)}) async-start(), calls=%async_computation.23 | async-start | bytes 1179648 | tf_op jit(solution)/shard_map/reduce_scatter | solution.py:282
  703.7 344.4 %reduce-scatter.23.cloned.1.call-start = ((), (), s32[]{:S(2)}) async-start(), calls=%async_computation.22 | async-start | bytes 1179648 | tf_op jit(solution)/shard_map/reduce_scatter | solution.py:281
  706.6 408.4 %reduce-scatter.21.cloned.1.call-start = ((), (), s32[]{:S(2)}) async-start(), calls=%async_computation.21 | async-start | bytes 1179648 | tf_op jit(solution)/shard_map/reduce_scatter | solution.py:280
  708.5 19.5 %copy-start.7 = (bf16[256,1024]{1,0:T(8,128)(2,1)S(1)}, bf16[256,1024]{1,0:T(8,128)(2,1)}, u32[]{:S(2)}) copy-start(bf16[256,1024]{1,0:T(8,128)(2,1)} %param.27) | copy-start | bytes 1572868
  708.5 19.5 %copy-start.35 = (f32[1024]{0:T(1024)S(1)}, f32[1024]{0:T(1024)}, u32[]{:S(2)}) copy-start(f32[1024]{0:T(1024)} %param.29) | copy-start | bytes 12292
  708.5 19.5 %copy-start.41 = (f32[256]{0:T(256)S(1)}, f32[256]{0:T(256)}, u32[]{:S(2)}) copy-start(f32[256]{0:T(256)} %copy-done.40) | copy-start | bytes 3076
  708.5 19.5 %copy-start.45 = (f32[256]{0:T(256)S(1)}, f32[256]{0:T(256)}, u32[]{:S(2)}) copy-start(f32[256]{0:T(256)} %copy-done.44) | copy-start | bytes 3076
  708.5 473.6 %reduce-scatter.19.cloned.1.call-start = ((), (), s32[]{:S(2)}) async-start(), calls=%async_computation.20 | async-start | bytes 1179648 | tf_op jit(solution)/shard_map/reduce_scatter | solution.py:279
  710.3 613.4 %all-reduce.4.cloned.1.call-start = ((), (), s32[]{:S(2)}) async-start(), calls=%async_computation.26 | async-start | bytes 181248 | tf_op jit(solution)/shard_map/psum | solution.py:301
  711.0 19.3 %copy-start.33 = (f32[4096]{0:T(1024)}, f32[4096]{0:T(1024)S(1)}, u32[]{:S(2)}) copy-start(f32[4096]{0:T(1024)S(1)} %dynamic_update_slice.34) | copy-start | bytes 49156
  711.3 19.0 %copy-start.34 = (f32[4096]{0:T(1024)}, f32[4096]{0:T(1024)S(1)}, u32[]{:S(2)}) copy-start(f32[4096]{0:T(1024)S(1)} %dynamic_update_slice.33) | copy-start | bytes 49156
  711.6 18.8 %copy-start.32 = (f32[4096]{0:T(1024)}, f32[4096]{0:T(1024)S(1)}, u32[]{:S(2)}) copy-start(f32[4096]{0:T(1024)S(1)} %dynamic_update_slice.32) | copy-start | bytes 49156
  713.4 17.0 %copy-start.50 = (f32[16]{0:T(128)}, f32[16]{0:T(128)S(1)}, u32[]{:S(2)}) copy-start(f32[16]{0:T(128)S(1)} %dynamic_update_slice.31) | copy-start | bytes 196
  713.6 16.7 %copy-start.43 = (f32[1024]{0:T(1024)}, f32[1024]{0:T(1024)S(1)}, u32[]{:S(2)}) copy-start(f32[1024]{0:T(1024)S(1)} %dynamic_update_slice.29) | copy-start | bytes 12292
  713.8 16.5 %copy-start.42 = (f32[1024]{0:T(1024)}, f32[1024]{0:T(1024)S(1)}, u32[]{:S(2)}) copy-start(f32[1024]{0:T(1024)S(1)} %dynamic_update_slice.30) | copy-start | bytes 12292
  (24 other events, 59.2 us)
Sparse Core Ops, SparseCore 0:
  12.6 25.2 all-gather.6
  192.9 44.0 reduce-scatter.10
  238.5 22.5 all-gather.14
  263.0 50.3 all-gather.12
  315.4 47.2 all-gather.10
  364.7 21.0 all-gather.8
  439.6 44.5 reduce-scatter.14
  486.7 44.5 reduce-scatter.12
  537.4 22.5 all-gather.16
  683.3 44.5 reduce-scatter.16
  732.2 88.3 reduce-scatter.26
  824.6 88.3 reduce-scatter.28
  916.9 64.2 reduce-scatter.24
  985.0 63.0 reduce-scatter.22
  1052.0 63.0 reduce-scatter.20
  1118.9 63.1 reduce-scatter.18
  1190.1 133.6 all-reduce.3
where the time goes:
time: 1360 us; the launch traced here: 1350 us
  waiting for transfers between devices  881 us (65%)
  matrix products  183 us (13%)
  blocking collectives  143 us (11%)
  local copies, waits for them, and re-layouts  65.3 us (5%)
  other arithmetic  52.2 us (4%)
  between operations  15.1 us (1%)
    psum x1, waiting for transfers between devices, per_device(): lax.psum((grad_ln1_gain, grad_ln1_bias, place_part(grad_b_query_here, ind...  142 us
    reduce_scatter x1, waiting for transfers between devices, per_device(): lax.psum_scatter(grad_down, 'dp', scatter_dimension=1, tiled=True)  92.4 us
    reduce_scatter x1, waiting for transfers between devices, per_device(): lax.psum_scatter(grad_up, 'dp', scatter_dimension=0, tiled=True)  87.3 us
    reduce_scatter x1, waiting for transfers between devices, per_device(): lax.psum_scatter(grad_out_w, 'dp', scatter_dimension=1, tiled=True)  68.2 us
    reduce_scatter x1, waiting for transfers between devices, per_device(): lax.psum_scatter(grad_query_w, 'dp', scatter_dimension=0, tiled=True)  67 us
    reduce_scatter x1, waiting for transfers between devices, per_device(): lax.psum_scatter(grad_key_w, 'dp', scatter_dimension=0, tiled=True)  67 us
    reduce_scatter x1, waiting for transfers between devices, per_device(): lax.psum_scatter(grad_value_w, 'dp', scatter_dimension=0, tiled=True)  66.9 us
    all_gather x1, waiting for transfers between devices, per_device(): lax.all_gather(w_down, 'dp', axis=1, tiled=True)  52.3 us
  transfers between devices with their start and end apart: 17, of which 16 were waited for; matrix products, arithmetic and copies ran while one was open for 5% of the time, Pallas kernels for 0%

commit v1 on v0

v1 whole, which is shorter than its diff:
```python
import functools

import jax
import jax.numpy as jnp
from jax import lax
from jax.experimental import pallas as pl
from jax.experimental.pallas import tpu as pltpu
from jax.sharding import PartitionSpec as P

D = 1024
HEADS = 16
HD = 64
FF = 4096
LONGEST = 512
EPS = 1e-05
SCALE = HD ** (-0.5)
F32 = jnp.float32
BF16 = jnp.bfloat16


def dot(left, right, left_dim=1, right_dim=0):
    return lax.dot_general(
        left, right, (((left_dim,), (right_dim,)), ((), ())), preferred_element_type=F32
    )


def norm_parts(values):
    mean = jnp.mean(values, axis=-1, keepdims=True)
    centered = values - mean
    inverse = lax.rsqrt(jnp.mean(centered * centered, axis=-1, keepdims=True) + EPS)
    return centered * inverse, inverse


def norm_backward(grad, unit, inverse, gain):
    scaled = grad * gain
    return inverse * (
        scaled
        - jnp.mean(scaled, axis=-1, keepdims=True)
        - unit * jnp.mean(scaled * unit, axis=-1, keepdims=True)
    )


def gelu_slope(values):
    normal_cdf = 0.5 * (1.0 + lax.erf(values * 0.7071067811865476))
    density = jnp.exp(-0.5 * values * values) * 0.3989422804014327
    return normal_cdf + values * density


def swap(value, axis, mask):
    size = lax.axis_size(axis)
    return lax.ppermute(value, axis, [(i, i ^ mask) for i in range(size)])


def bit_of(axis, mask):
    return (lax.axis_index(axis) // mask) % 2


def join(mine, other, bit, axis):
    return jnp.where(
        bit == 0, jnp.stack([mine, other], axis), jnp.stack([other, mine], axis)
    )


def gather_shards(shard, axis):
    size = lax.axis_size(axis)
    shape = shard.shape
    mask, steps = size // 2, 0
    while mask:
        shard = join(shard, swap(shard, axis, mask), bit_of(axis, mask), steps)
        mask, steps = mask // 2, steps + 1
    return shard.reshape((size,) + shape)


def pick_cols(value, width, bit):
    rows, cols = value.shape
    pairs = cols // (2 * width)
    if width % 128:
        return lax.dynamic_index_in_dim(
            value.reshape(rows, pairs, 2, width), bit, 2, keepdims=False
        ).reshape(rows, pairs * width)
    return jnp.concatenate(
        [
            lax.dynamic_slice_in_dim(value, (2 * p + bit) * width, width, 1)
            for p in range(pairs)
        ],
        1,
    )


def pick_rows(value, height, bit):
    rows, cols = value.shape
    return lax.dynamic_index_in_dim(
        value.reshape(rows // (2 * height), 2, height, cols), bit, 1, keepdims=False
    ).reshape(rows // 2, cols)


def scatter_sum(send, keep, axis, pick, extent):
    size = lax.axis_size(axis)
    total = keep + swap(send, axis, 1).astype(F32)
    mask = 2
    while mask < size:
        bit = bit_of(axis, mask)
        other = swap(pick(total, extent, 1 - bit).astype(BF16), axis, mask)
        total = pick(total, extent, bit) + other.astype(F32)
        mask *= 2
    return total


def sum_everywhere(value):
    for axis in ("tensor", "dp"):
        mask = 1
        while mask < lax.axis_size(axis):
            value = value + swap(value, axis, mask)
            mask *= 2
    return value


def key_range(block, size):
    low = max(0, block * size - (LONGEST // size) * size)
    return low, (block + 1) * size - low


def write_bias(bias_ref, seg_col_ref, seg_row_ref, block, size):
    low, count = key_range(block, size)
    key_pos = low + lax.broadcasted_iota(jnp.int32, (count, size), 0)
    row_pos = block * size + lax.broadcasted_iota(jnp.int32, (count, size), 1)
    same = seg_col_ref[low : low + count, :] == seg_row_ref[:, block * size : (block + 1) * size]
    bias_ref[:count, :] = jnp.where((key_pos <= row_pos) & same, 0.0, -1000000000.0)


def attend_kernel(size, qkv_ref, seg_col_ref, seg_row_ref, scale_ref, o_ref, u_ref, lse_ref,
                  bias_ref, vt_ref, ot_ref):
    length, width = o_ref.shape
    heads = width // HD
    vt_ref[...] = qkv_ref[:, 2 * width :].astype(F32).T.astype(BF16)
    head_of = lax.broadcasted_iota(jnp.int32, (size, width), 1) // HD
    for block in range(length // size):
        low, count = key_range(block, size)
        write_bias(bias_ref, seg_col_ref, seg_row_ref, block, size)
        query = qkv_ref[block * size : (block + 1) * size, :width].astype(F32) * SCALE
        keys = qkv_ref[low : low + count, width : 2 * width]

        def one_head(head, carry):
            masked = jnp.where(head_of == head, query, 0.0).astype(BF16)
            scores = dot(keys, masked, 1, 1) + bias_ref[:count, :]
            highest = jnp.max(scores, axis=0, keepdims=True)
            raised = jnp.exp(scores - highest)
            total = jnp.sum(raised, axis=0, keepdims=True)
            lse_ref[pl.ds(block * heads + head, 1), :] = highest + jnp.log(total)
            probs = (raised * (1.0 / total)).astype(BF16)
            row = pl.multiple_of(head * HD, HD)
            ot_ref[pl.ds(row, HD), :] = dot(vt_ref[pl.ds(row, HD), low : low + count], probs)
            return carry

        lax.fori_loop(0, heads, one_head, 0)
        mixed = ot_ref[...].T
        o_ref[block * size : (block + 1) * size, :] = mixed
        u_ref[block * size : (block + 1) * size, :] = (mixed * scale_ref[...]).astype(BF16)


def attend_back_kernel(size, qkv_ref, du_ref, o_ref, lse_ref, seg_col_ref, seg_row_ref, scale_ref,
                       dqkv_ref, sums_ref,
                       bias_ref, kt_ref, dqt_ref, probs_ref, ds_ref, q_ref, do_ref, dk_ref, dv_ref):
    length, width = o_ref.shape
    heads = width // HD
    kt_ref[...] = qkv_ref[:, width : 2 * width].astype(F32).T.astype(BF16)
    dk_ref[...] = jnp.zeros_like(dk_ref)
    dv_ref[...] = jnp.zeros_like(dv_ref)
    head_of = lax.broadcasted_iota(jnp.int32, (size, width), 1) // HD
    scale_sum = jnp.zeros((1, width), F32)
    bias_sum = jnp.zeros((1, width), F32)
    for block in range(length // size):
        low, count = key_range(block, size)
        rows = slice(block * size, (block + 1) * size)
        write_bias(bias_ref, seg_col_ref, seg_row_ref, block, size)
        query = qkv_ref[rows, :width].astype(F32) * SCALE
        keys = qkv_ref[low : low + count, width : 2 * width]
        values = qkv_ref[low : low + count, 2 * width :]
        du = du_ref[rows, :]
        scale_sum = scale_sum + jnp.sum(du * o_ref[rows, :], axis=0, keepdims=True)
        grad = du * scale_ref[...]

        def one_head(head, carry):
            masked = jnp.where(head_of == head, query, 0.0).astype(BF16)
            grad_here = jnp.where(head_of == head, grad, 0.0).astype(BF16)
            here = pl.ds(pl.multiple_of(head * size, size), size)
            q_ref[here, :] = masked
            do_ref[here, :] = grad_here
            scores = dot(keys, masked, 1, 1) + bias_ref[:count, :]
            full = jnp.exp(scores - lse_ref[pl.ds(block * heads + head, 1), :])
            probs_ref[:count, here] = full.astype(BF16)
            dp = dot(values, grad_here, 1, 1)
            delta = jnp.sum(full * dp, axis=0, keepdims=True)
            ds = (full * (dp - delta)).astype(BF16)
            ds_ref[:count, here] = ds
            row = pl.multiple_of(head * HD, HD)
            dqt_ref[pl.ds(row, HD), :] = dot(kt_ref[pl.ds(row, HD), low : low + count], ds)
            return carry

        lax.fori_loop(0, heads, one_head, 0)
        dq = (dqt_ref[...].T * SCALE).astype(BF16)
        dqkv_ref[rows, :width] = dq
        bias_sum = bias_sum + jnp.sum(dq.astype(F32), axis=0, keepdims=True)
        dk_ref[low : low + count, :] += dot(ds_ref[:count, :], q_ref[...])
        dv_ref[low : low + count, :] += dot(probs_ref[:count, :], do_ref[...])
    dqkv_ref[:, width : 2 * width] = dk_ref[...].astype(BF16)
    dv = dv_ref[...].astype(BF16)
    dqkv_ref[:, 2 * width :] = dv
    sums_ref[0:1, :] = bias_sum
    sums_ref[1:2, :] = jnp.sum(dv.astype(F32), axis=0, keepdims=True)
    sums_ref[2:3, :] = scale_sum
    sums_ref[3:8, :] = jnp.zeros((5, width), F32)


def whole(count):
    return [pl.BlockSpec(memory_space=pltpu.VMEM)] * count


def attend(qkv, seg_col, seg_row, scale_row):
    length, width = qkv.shape[0], qkv.shape[1] // 3
    size = 256
    blocks, heads = length // size, width // HD
    most = LONGEST + size
    cost = blocks * heads * most * size
    return pl.pallas_call(
        functools.partial(attend_kernel, size),
        out_shape=(
            jax.ShapeDtypeStruct((length, width), F32),
            jax.ShapeDtypeStruct((length, width), BF16),
            jax.ShapeDtypeStruct((blocks * heads, size), F32),
        ),
        in_specs=whole(4),
        out_specs=tuple(whole(3)),
        scratch_shapes=[
            pltpu.VMEM((most, size), F32),
            pltpu.VMEM((width, length), BF16),
            pltpu.VMEM((width, size), F32),
        ],
        cost_estimate=pl.CostEstimate(
            flops=cost * 4 * width, bytes_accessed=length * width * 12, transcendentals=cost
        ),
        name="attend",
    )(qkv, seg_col, seg_row, scale_row)


def attend_back(qkv, du, mixed, lse, seg_col, seg_row, scale_row):
    length, width = mixed.shape
    size = 256
    blocks, heads = length // size, width // HD
    most = LONGEST + size
    cost = blocks * heads * most * size
    return pl.pallas_call(
        functools.partial(attend_back_kernel, size),
        out_shape=(
            jax.ShapeDtypeStruct((length, 3 * width), BF16),
            jax.ShapeDtypeStruct((8, width), F32),
        ),
        in_specs=whole(7),
        out_specs=tuple(whole(2)),
        scratch_shapes=[
            pltpu.VMEM((most, size), F32),
            pltpu.VMEM((width, length), BF16),
            pltpu.VMEM((width, size), F32),
            pltpu.VMEM((most, heads * size), BF16),
            pltpu.VMEM((most, heads * size), BF16),
            pltpu.VMEM((heads * size, width), BF16),
            pltpu.VMEM((heads * size, width), BF16),
            pltpu.VMEM((length, width), F32),
            pltpu.VMEM((length, width), F32),
        ],
        cost_estimate=pl.CostEstimate(
            flops=cost * 10 * width, bytes_accessed=length * width * 20, transcendentals=cost
        ),
        name="attend_back",
    )(qkv, du, mixed, lse, seg_col, seg_row, scale_row)


def per_device(
    tokens,
    segments,
    ln1_gain,
    ln1_bias,
    w_query,
    b_query,
    w_key,
    w_value,
    b_value,
    head_scale,
    w_out,
    b_out,
    post_gain,
    post_bias,
    ln2_gain,
    ln2_bias,
    w_up,
    b_up,
    ffn_gain,
    ffn_bias,
    w_down,
    b_down,
    cotangent,
):
    index = lax.axis_index("tensor")
    side, half = index % 2, index // 2
    rows = tokens.shape[0]
    length = rows * lax.axis_size("tensor")
    columns = w_query.shape[1]
    hidden_here = w_up.shape[1]
    near = bit_of("dp", 1)

    def own_part(vector, width):
        return lax.dynamic_slice_in_dim(vector, index * width, width, 0)

    def pair_rows(value):
        return join(value, swap(value, "tensor", 2), half, 0)

    def all_rows(pair):
        full = join(pair, swap(pair, "tensor", 1), side, 1)
        return full.reshape((length,) + pair.shape[2:])

    def side_rows(value, which):
        picked = lax.dynamic_index_in_dim(
            value.reshape((2, 2, rows) + value.shape[1:]), which, 1, keepdims=False
        )
        return picked.reshape((2 * rows,) + value.shape[1:])

    def side_sum(left, right, right_dim):
        send = dot(side_rows(left, 1 - side), right, 1, right_dim).astype(BF16)
        other = swap(send, "tensor", 1)
        return dot(side_rows(left, side), right, 1, right_dim) + other.astype(F32)

    def half_sum(part):
        part = part.reshape(2, rows, D)
        send = lax.dynamic_index_in_dim(part, 1 - half, 0, keepdims=False).astype(BF16)
        keep = lax.dynamic_index_in_dim(part, half, 0, keepdims=False)
        return keep + swap(send, "tensor", 2).astype(F32)

    x_pair = pair_rows(tokens)
    x_all = all_rows(x_pair)
    qkv_w = gather_shards(jnp.concatenate([w_query, w_key, w_value], 1), "dp").reshape(
        D, 3 * columns
    )
    out_w = jnp.moveaxis(gather_shards(w_out, "dp"), 0, 1).reshape(columns, D)
    up_w = gather_shards(w_up, "dp").reshape(D, hidden_here)
    down_w = jnp.moveaxis(gather_shards(w_down, "dp"), 0, 1).reshape(hidden_here, D)
    g_pair = pair_rows(cotangent)
    g_all = all_rows(g_pair)

    segment = segments[0]
    seg_col, seg_row = segment[:, None], segment[None, :]
    scale_row = jnp.repeat(own_part(head_scale, columns // HD), HD)[None, :]
    shard = D // lax.axis_size("dp")

    unit_all, _ = norm_parts(x_all.astype(F32))
    normed = (unit_all * ln1_gain + ln1_bias).astype(BF16)
    qkv_b = jnp.concatenate(
        [own_part(b_query, columns), jnp.zeros((columns,), F32), own_part(b_value, columns)]
    )
    qkv = (dot(normed, qkv_w) + qkv_b).astype(BF16)
    mixed, scaled, lse = attend(qkv, seg_col, seg_row, scale_row)
    part = side_sum(scaled, out_w, 0)
    projected = part + swap(part.astype(BF16), "tensor", 2).astype(F32) + b_out
    unit_two, inverse_two = norm_parts(projected)
    hidden = x_pair.reshape(2 * rows, D).astype(F32) + (unit_two * post_gain + post_bias)
    unit_three, inverse_three = norm_parts(hidden)
    ffn_in = (unit_three * ln2_gain + ln2_bias).astype(BF16)
    ffn_all = all_rows(ffn_in.reshape(2, rows, D))

    gain_here, shift_here = own_part(ffn_gain, hidden_here), own_part(ffn_bias, hidden_here)
    grad_inner = dot(g_all, down_w, 1, 1)
    scaled_grad = grad_inner * gain_here
    before = dot(ffn_all, up_w) + own_part(b_up, hidden_here)
    active = jax.nn.gelu(before, approximate=False)
    mean = jnp.mean(active, axis=-1)
    off_mean = active - mean[:, None]
    square = jnp.sum(off_mean * off_mean, axis=-1)
    plain = jnp.sum(scaled_grad, axis=-1)
    cross = jnp.sum(scaled_grad * off_mean, axis=-1)
    stats = jnp.stack([mean, square, plain, cross])
    count = hidden_here
    for mask in (1, 2):
        other = swap(stats, "tensor", mask)
        middle = 0.5 * (stats[0] + other[0])
        gap = stats[0] - other[0]
        stats = jnp.stack(
            [
                middle,
                stats[1] + other[1] + (0.5 * count) * gap * gap,
                stats[2] + other[2],
                stats[3]
                + other[3]
                + ((stats[0] - middle) * stats[2] + (other[0] - middle) * other[2]),
            ]
        )
        count *= 2
    mean, square, plain, cross = (stats[i][:, None] for i in range(4))
    inverse_four = lax.rsqrt(square / FF + EPS)
    unit_four = (active - mean) * inverse_four
    inner = (unit_four * gain_here + shift_here).astype(BF16)
    grad_active = inverse_four * (
        scaled_grad - plain / FF - unit_four * (cross * inverse_four / FF)
    )
    grad_before = (grad_active * gelu_slope(before)).astype(BF16)

    part = side_sum(grad_before, up_w, 1)
    grad_ffn_in = part + swap(part.astype(BF16), "tensor", 2).astype(F32)
    grad_hidden = g_pair.reshape(2 * rows, D).astype(F32) + norm_backward(
        grad_ffn_in, unit_three, inverse_three, ln2_gain
    )
    grad_proj = norm_backward(grad_hidden, unit_two, inverse_two, post_gain).astype(BF16)
    grad_proj_all = all_rows(grad_proj.reshape(2, rows, D))

    grad_scaled = dot(grad_proj_all, out_w, 1, 1)
    grad_qkv, sums = attend_back(qkv, grad_scaled, mixed, lse, seg_col, seg_row, scale_row)
    grad_normed = half_sum(side_sum(grad_qkv, qkv_w, 1))
    unit_one, inverse_one = norm_parts(tokens.astype(F32))
    own_grad_hidden = lax.dynamic_index_in_dim(
        grad_hidden.reshape(2, rows, D), half, 0, keepdims=False
    )
    input_grad = own_grad_hidden + norm_backward(grad_normed, unit_one, inverse_one, ln1_gain)

    own_hidden = lax.dynamic_index_in_dim(hidden.reshape(2, rows, D), half, 0, keepdims=False)
    branch = half_sum(side_sum(inner, down_w, 0))
    output = (own_hidden + (branch + b_down)).astype(BF16)

    def down_part(bit):
        return dot(inner, pick_cols(g_all, shard, bit), 0, 0)

    g_down_w = scatter_sum(
        down_part(1 - near).astype(BF16), down_part(near), "dp", pick_cols, shard
    )

    def up_part(bit):
        return dot(pick_cols(ffn_all, shard, bit), grad_before, 0, 0)

    g_up_w = scatter_sum(up_part(1 - near).astype(BF16), up_part(near), "dp", pick_rows, shard)

    def out_part(bit):
        return dot(scaled, pick_cols(grad_proj_all, shard, bit), 0, 0)

    g_out_w = scatter_sum(out_part(1 - near).astype(BF16), out_part(near), "dp", pick_cols, shard)

    def qkv_part(bit):
        return dot(pick_cols(normed, shard, bit), grad_qkv, 0, 0)

    g_qkv_w = scatter_sum(qkv_part(1 - near).astype(BF16), qkv_part(near), "dp", pick_rows, shard)

    def columns_sum(value):
        return jnp.sum(value, axis=0)

    def place(vector, width, count_rows):
        return lax.dynamic_update_slice_in_dim(
            jnp.zeros((count_rows * D,), F32), vector, index * width, 0
        ).reshape(count_rows, D)

    early = jnp.concatenate(
        [
            jnp.stack(
                [
                    columns_sum(cotangent.astype(F32)),
                    0.5 * columns_sum(grad_ffn_in * unit_three),
                    0.5 * columns_sum(grad_ffn_in),
                    0.5 * columns_sum(grad_hidden * unit_two),
                    0.5 * columns_sum(grad_hidden),
                    0.5 * columns_sum(grad_proj.astype(F32)),
                ]
            ),
            place(columns_sum(grad_before.astype(F32)), hidden_here, FF // D),
            place(columns_sum(grad_inner * unit_four), hidden_here, FF // D),
            place(columns_sum(grad_inner), hidden_here, FF // D),
        ]
    )
    early = sum_everywhere(early)
    heads_sum = jnp.sum(sums[2].reshape(columns // HD, HD), axis=1)
    late = jnp.concatenate(
        [
            jnp.stack([columns_sum(grad_normed * unit_one), columns_sum(grad_normed)]),
            place(sums[0], columns, 1),
            place(sums[1], columns, 1),
            place(heads_sum, columns // HD, 1),
        ]
    )
    late = sum_everywhere(late)
    blocks = FF // D
    return (
        output,
        input_grad,
        late[0],
        late[1],
        g_qkv_w[:, :columns],
        late[2],
        g_qkv_w[:, columns : 2 * columns],
        g_qkv_w[:, 2 * columns :],
        late[3],
        late[4, :HEADS],
        g_out_w,
        early[5],
        early[3],
        early[4],
        early[1],
        early[2],
        g_up_w,
        early[6 : 6 + blocks].reshape(FF),
        early[6 + blocks : 6 + 2 * blocks].reshape(FF),
        early[6 + 2 * blocks : 6 + 3 * blocks].reshape(FF),
        g_down_w,
        early[0],
    )


def solution(mesh):
    return jax.shard_map(
        per_device,
        mesh=mesh,
        in_specs=(
            P(("dp", "tensor"), None),
            P("dp", None),
            P(),
            P(),
            P("dp", "tensor"),
            P(),
            P("dp", "tensor"),
            P("dp", "tensor"),
            P(),
            P(),
            P("tensor", "dp"),
            P(),
            P(),
            P(),
            P(),
            P(),
            P("dp", "tensor"),
            P(),
            P(),
            P(),
            P("tensor", "dp"),
            P(),
            P(("dp", "tensor"), None),
        ),
        out_specs=(
            P(("dp", "tensor"), None),
            P(("dp", "tensor"), None),
            P(),
            P(),
            P("dp", "tensor"),
            P(),
            P("dp", "tensor"),
            P("dp", "tensor"),
            P(),
            P(),
            P("tensor", "dp"),
            P(),
            P(),
            P(),
            P(),
            P(),
            P("dp", "tensor"),
            P(),
            P(),
            P(),
            P("tensor", "dp"),
            P(),
        ),
        check_vma=False,
    )
```

time: 1360 us -> 423 us (0.31)
  waiting for transfers between devices: 881 us -> 168 us
  blocking collectives: 143 us -> 0 us
  matrix products: 183 us -> 63.8 us
  starting transfers between devices: 0.91 us -> 38.2 us
  Pallas kernels: 0 us -> 32.5 us
  local copies, waits for them, and re-layouts: 65.3 us -> 43.7 us
  other arithmetic: 52.2 us -> 69.5 us
    reduce_scatter x10 -> x0, waiting for transfers between devices: 586 us -> none  [the longest x1 92.4 us: per_device(): lax.psum_scatter(grad_down, 'dp', scatter_dimension=1, tiled=True)]
    ppermute x0 -> x50, waiting for transfers between devices: none -> 168 us  [swap(): return lax.ppermute(value, axis, [(i, i ^ mask) for i in range(size)])]
    all_gather x6 -> x0, waiting for transfers between devices: 151 us -> none  [the longest x1 52.3 us: per_device(): lax.all_gather(w_down, 'dp', axis=1, tiled=True)]
    psum x1 -> x0, waiting for transfers between devices: 142 us -> none  [per_device(): lax.psum((grad_ln1_gain, grad_ln1_bias, place_part(grad_b_query_here, ind...]
    all_gather x4 -> x0, blocking collectives: 124 us -> none  [the longest x1 33.3 us: per_device(): lax.all_gather(w_query, 'dp', axis=0, tiled=True)]
    dot_general x32 -> x20, matrix products: 183 us -> 63.8 us  [dot(): lax.dot_general(left, right, (((left_dim,), (right_dim,)), ((), ())), pre...]
    ppermute x0 -> x50, starting transfers between devices: none -> 38.2 us  [swap(): return lax.ppermute(value, axis, [(i, i ^ mask) for i in range(size)])]
    pallas_call x0 -> x2, Pallas kernels: none -> 32.5 us  [the longest x1 18 us: attend_back(): pl.pallas_call(functools.partial(attend_back_kernel, size), out_shape=(ja...]
  transfers between devices with their start and end apart: 17 -> 50, of which waited for: 16 -> 23; matrix products, arithmetic and copies ran while one was open for 5% -> 30% of each run, Pallas kernels for 0% -> 8%
where the time goes in v1:
time: 423 us; the launch traced here: 418 us
  waiting for transfers between devices  168 us (40%)
  other arithmetic  69.5 us (16%)
  matrix products  63.8 us (15%)
  local copies, waits for them, and re-layouts  43.7 us (10%)
  starting transfers between devices  38.2 us (9%)
  Pallas kernels  32.5 us (8%)
    ppermute x50, waiting for transfers between devices, swap(): return lax.ppermute(value, axis, [(i, i ^ mask) for i in range(size)])  168 us
    dot_general x20, matrix products, dot(): lax.dot_general(left, right, (((left_dim,), (right_dim,)), ((), ())), pre...  63.8 us
    ppermute x50, starting transfers between devices, swap(): return lax.ppermute(value, axis, [(i, i ^ mask) for i in range(size)])  38.2 us
    select_n x27, other arithmetic, join(): jnp.where(bit == 0, jnp.stack([mine, other], axis), jnp.stack([other, min...  24.7 us
    pallas_call x1, Pallas kernels, attend_back(): pl.pallas_call(functools.partial(attend_back_kernel, size), out_shape=(ja...  18 us
    reduce_sum x6, other arithmetic, columns_sum(): return jnp.sum(value, axis=0)  15.8 us
    pallas_call x1, Pallas kernels, attend(): pl.pallas_call(functools.partial(attend_kernel, size), out_shape=(jax.Sha...  14.5 us
    unnamed x163, local copies, waits for them, and re-layouts  8.7 us
  transfers between devices with their start and end apart: 50, of which 23 were waited for; matrix products, arithmetic and copies ran while one was open for 30% of the time, Pallas kernels for 8%

profile of v1, /device:TPU:0, one launch (start us, length us, event | category | flops | bytes accessed | tf_op | source)
XLA Modules:
  0.0 418.2 jit_solution(2412891700689753729)
XLA Ops:
  0.7 4.1 collective-permute-start.5
  9.2 2.6 collective-permute-start.11
  23.9 9.0 %collective-permute-done.6 = bf16[2,256,128]{2,1,0:T(8,128)(2,1)S(1)} collective-permute-done((bf16[2,256,128]{2,1,0:T(8,128)(2,1)S(1)}, bf16[2,256,128]{2,1,0:T(8,128)(2,1)S(1)}, u32[]{:S(2)}, u32[]{:S(2)}) %collective-permute-start.6) | collective-permute-done | bytes 131104 | tf_op jit(solution)/shard_map/ppermute | solution.py:51
  35.9 9.5 %collective-permute-done.3 = bf16[2,128,768]{2,1,0:T(8,128)(2,1)S(1)} collective-permute-done((bf16[2,128,768]{2,1,0:T(8,128)(2,1)S(1)}, bf16[2,128,768]{2,1,0:T(8,128)(2,1)S(1)}, u32[]{:S(2)}, u32[]{:S(2)}) %collective-permute-start.3) | collective-permute-done | bytes 393248 | tf_op jit(solution)/shard_map/ppermute | solution.py:51
  50.6 14.5 %collective-permute-done.4 = bf16[2,2,128,768]{3,2,1,0:T(8,128)(2,1)} collective-permute-done((bf16[2,2,128,768]{3,2,1,0:T(8,128)(2,1)}, bf16[2,2,128,768]{3,2,1,0:T(8,128)(2,1)}, u32[]{:S(2)}, u32[]{:S(2)}) %collective-permute-start.4) | collective-permute-done | bytes 786464 | tf_op jit(solution)/shard_map/ppermute | solution.py:51
  69.7 3.0 add_convert_fusion.2.qkv_ref
  72.7 14.5 %attend.1 = (f32[1024,256]{1,0:T(8,128)}, bf16[1024,256]{1,0:T(8,128)(2,1)}, f32[16,256]{1,0:T(8,128)}) custom-call(bf16[1024,768]{1,0:T(8,128)(2,1)} %add_convert_fusion.2.qkv_ref, s32[1024,1]{1,0:T(8,128)} %copy.62.seg_col_ref, s32[1,1024]{1,0:T(1,128)} %seg_row_ref.3, f32[1,256]{1,0:T(1,128)} %broadcast_in_dim_reshape.3.scale_ref), custom_call_target="tpu_custom_call" | custom-call | flops 3221225472 | bytes 3145728 | tf_op jit(solution)/shard_map/attend/pallas_call | solution.py:225
  101.0 3.9 collective-permute-done.12
  108.7 7.0 %collective-permute-done.17 = bf16[2,1024,128]{2,1,0:T(8,128)(2,1)S(1)} collective-permute-done((bf16[2,1024,128]{2,1,0:T(8,128)(2,1)S(1)}, bf16[2,1024,128]{2,1,0:T(8,128)(2,1)S(1)}, u32[]{:S(2)}, u32[]{:S(2)}) %collective-permute-start.17) | collective-permute-done | bytes 524320 | tf_op jit(solution)/shard_map/ppermute | solution.py:51
  118.0 13.1 %collective-permute-done.9 = bf16[512,1024]{1,0:T(8,128)(2,1)S(1)} collective-permute-done((bf16[512,1024]{1,0:T(8,128)(2,1)S(1)}, bf16[512,1024]{1,0:T(8,128)(2,1)S(1)}, u32[]{:S(2)}, u32[]{:S(2)}) %collective-permute-start.9) | collective-permute-done | bytes 1048608 | tf_op jit(solution)/shard_map/ppermute | solution.py:51
  132.3 1.9 fusion.128
  138.2 2.7 fusion.11
  140.9 12.0 %collective-permute-done.18 = bf16[2,2,1024,128]{3,2,1,0:T(8,128)(2,1)S(1)} collective-permute-done((bf16[2,2,1024,128]{3,2,1,0:T(8,128)(2,1)S(1)}, bf16[2,2,1024,128]{3,2,1,0:T(8,128)(2,1)S(1)}, u32[]{:S(2)}, u32[]{:S(2)}) %collective-permute-start.18) | collective-permute-done | bytes 1048608 | tf_op jit(solution)/shard_map/ppermute | solution.py:51
  154.7 4.0 copy.72
  160.6 3.3 maximum_select_fusion.1
  164.1 23.5 %fusion.126 = (f32[1024]{0:T(1024)S(1)}, f32[1024,1024]{1,0:T(8,128)S(1)}, f32[1024,1024]{1,0:T(8,128)}) fusion(f32[1024]{0:T(1024)S(1)} %dynamic_slice.230, bf16[1024,1024]{1,0:T(8,128)(2,1)S(1)} %bitcast.241, bf16[1024,1024]{1,0:T(8,128)(2,1)S(1)} %bitcast.268), kind=kOutput, calls=%fused_computation.327 | convolution fusion | flops 2216688640 | bytes 12591104 | tf_op jit(solution)/shard_map/dot_general | solution.py:22
  187.6 4.8 %multiply_reduce_fusion.2 = (f32[1024]{0:T(1024)S(1)}, f32[1024]{0:T(1024)S(1)}, f32[1024]{0:T(1024)S(1)}, f32[1024]{0:T(1024)S(1)}, f32[1024,1024]{1,0:T(8,128)}) fusion(f32[1024,1024]{1,0:T(8,128)S(1)} %get-tuple-element.102, f32[1024]{0:T(1024)S(1)} %broadcast_multiply_fusion.5, f32[1024]{0:T(1024)S(1)} %dynamic_slice.231, ...), kind=kOutput, calls=%fused_computation.20 | convolution fusion | flops 2155868160 | bytes 12607488 | tf_op jit(solution)/shard_map/dot_general | solution.py:22
  195.7 2.3 constant_dynamic-slice_fusion.9
  198.4 7.1 %convert_reduce_fusion = (f32[1024]{0:T(1024)S(1)}, bf16[1024,1024]{1,0:T(8,128)(2,1)S(1)}, f32[1024]{0:T(1024)S(1)}, bf16[1024,1024]{1,0:T(8,128)(2,1)S(1)}) fusion(f32[1024,1024]{1,0:T(8,128)} %get-tuple-element.203, f32[1024]{0:T(1024)S(1)} %dynamic_slice.230, f32[1024]{0:T(1024)S(1)} %get-tuple-element.99, f32[1024,1024]{1,0:T(8,128)} %copy-done.17, ...), kind=kLoop, calls=%fused_computation.16 | loop fusion | flops 26212352 | bytes 16814080 | tf_op jit(solution)/shard_map/reduce_sum | solution.py:449
  205.6 2.3 convolution_convert_fusion.1
  208.4 2.3 convolution_convert_fusion.2
  213.8 2.3 convolution_convert_fusion.3
  220.7 13.6 %collective-permute-done.47 = bf16[1024,512]{0,1:T(8,128)(2,1)} collective-permute-done((bf16[1024,512]{0,1:T(8,128)(2,1)}, bf16[1024,512]{0,1:T(8,128)(2,1)}, u32[]{:S(2)}, u32[]{:S(2)}) %collective-permute-start.47) | collective-permute-done | bytes 1048608 | tf_op jit(solution)/shard_map/ppermute | solution.py:51
  234.3 2.6 convert_add_fusion.2
  237.7 18.2 %collective-permute-done.44 = bf16[512,1024]{1,0:T(8,128)(2,1)} collective-permute-done((bf16[512,1024]{1,0:T(8,128)(2,1)}, bf16[512,1024]{1,0:T(8,128)(2,1)}, u32[]{:S(2)}, u32[]{:S(2)}) %collective-permute-start.44) | collective-permute-done | bytes 1048608 | tf_op jit(solution)/shard_map/ppermute | solution.py:51
  256.0 2.6 convert_add_fusion.3
  260.1 2.5 fusion.20
  271.1 17.6 %collective-permute-done.24 = bf16[512,1024]{1,0:T(8,128)(2,1)S(1)} collective-permute-done((bf16[512,1024]{1,0:T(8,128)(2,1)S(1)}, bf16[512,1024]{1,0:T(8,128)(2,1)S(1)}, u32[]{:S(2)}, u32[]{:S(2)}) %collective-permute-start.24) | collective-permute-done | bytes 1048608 | tf_op jit(solution)/shard_map/ppermute | solution.py:51
  288.7 2.5 multiply_reduce_fusion.6
  291.2 2.2 multiply_reduce_fusion.5
  302.7 2.6 collective-permute-done.40
  305.9 2.1 fusion.100
  312.6 5.2 %collective-permute-done.42 = f32[18,1024]{1,0:T(8,128)S(1)} collective-permute-done((f32[18,1024]{1,0:T(8,128)S(1)}, f32[18,1024]{1,0:T(8,128)S(1)}, u32[]{:S(2)}, u32[]{:S(2)}) %collective-permute-start.42) | collective-permute-done | bytes 73760 | tf_op jit(solution)/shard_map/ppermute | solution.py:51
  319.7 5.1 %collective-permute-done.43 = f32[18,1024]{1,0:T(8,128)S(1)} collective-permute-done((f32[18,1024]{1,0:T(8,128)S(1)}, f32[18,1024]{1,0:T(8,128)S(1)}, u32[]{:S(2)}, u32[]{:S(2)}) %collective-permute-start.43) | collective-permute-done | bytes 73760 | tf_op jit(solution)/shard_map/ppermute | solution.py:51
  334.2 18.0 %attend_back.1 = (bf16[1024,768]{1,0:T(8,128)(2,1)}, f32[8,256]{1,0:T(8,128)}) custom-call(bf16[1024,768]{1,0:T(8,128)(2,1)} %add_convert_fusion.2.qkv_ref, f32[1024,256]{1,0:T(8,128)} %fusion.134.du_ref, f32[1024,256]{1,0:T(8,128)} %get-tuple-element.28.o_ref, f32[16,256]{1,0:T(8,128)} %get-tuple-element.29.lse_ref, s32[1024,1]{1,0:T(8,128)} %copy.62.seg_col_ref, ...), custom_call_target="tpu_custom_call" | custom-call | flops 8053063680 | bytes 5242880 | tf_op jit(solution)/shard_map/attend_back/pallas_call | solution.py:252
  352.2 3.5 convolution_convert_fusion.6
  358.2 2.0 convolution_convert_fusion
  366.3 3.9 collective-permute-done.37
  372.0 3.2 collective-permute-done.33
  375.2 2.5 convert_add_fusion.9
  377.8 2.2 convert_add_fusion.4
  381.0 6.7 %collective-permute-done.34 = bf16[256,768]{1,0:T(8,128)(2,1)S(1)} collective-permute-done((bf16[256,768]{1,0:T(8,128)(2,1)S(1)}, bf16[256,768]{1,0:T(8,128)(2,1)S(1)}, u32[]{:S(2)}, u32[]{:S(2)}) %collective-permute-start.34) | collective-permute-done | bytes 393248 | tf_op jit(solution)/shard_map/ppermute | solution.py:51
  389.3 3.7 collective-permute-done.27
  394.7 4.1 collective-permute-done.35
  400.6 3.1 collective-permute-done.29
  405.2 2.4 collective-permute-done.30
  407.7 4.2 %collective-permute-done.31 = f32[5,1024]{1,0:T(8,128)S(1)} collective-permute-done((f32[5,1024]{1,0:T(8,128)S(1)}, f32[5,1024]{1,0:T(8,128)S(1)}, u32[]{:S(2)}, u32[]{:S(2)}) %collective-permute-start.31) | collective-permute-done | bytes 20512 | tf_op jit(solution)/shard_map/ppermute | solution.py:51
  413.4 3.3 collective-permute-done.32
  (396 shorter events, 126.2 us)
Async XLA Ops:
  0.7 21.5 %collective-permute-start.5 = (bf16[256,128]{1,0:T(8,128)(2,1)}, bf16[256,128]{1,0:T(8,128)(2,1)S(1)}, u32[]{:S(2)}, u32[]{:S(2)}) collective-permute-start(bf16[256,128]{1,0:T(8,128)(2,1)} %param.33), channel_id=1, source_target_pairs={{0,16},{4,20},{8,24},{12,28},{16,0},{20,4},{24,8},{28,12},{1,17},{... | collective-permute-start | bytes 196616 | tf_op jit(solution)/shard_map/ppermute | solution.py:51
  7.3 27.1 %collective-permute-start.2 = (bf16[128,768]{1,0:T(8,128)(2,1)S(1)}, bf16[128,768]{1,0:T(8,128)(2,1)S(1)}, u32[]{:S(2)}, u32[]{:S(2)}) collective-permute-start(bf16[128,768]{1,0:T(8,128)(2,1)S(1)} %constant_dynamic-update-slice_fusion.2), channel_id=1, source_target_pairs={{0,16},{4,20},{8,24},{12,28},{16,0},{20,4},{24,8},{28,12},{1,17},{... | collective-permute-start | bytes 589832 | tf_op jit(solution)/shard_map/ppermute | solution.py:51
  7.4 27.3 %collective-permute-start = (bf16[256,1024]{1,0:T(8,128)(2,1)}, bf16[256,1024]{1,0:T(8,128)(2,1)S(1)}, u32[]{:S(2)}, u32[]{:S(2)}) collective-permute-start(bf16[256,1024]{1,0:T(8,128)(2,1)} %param.23), channel_id=1, source_target_pairs={{0,2},{1,3},{2,0},{3,1},{4,6},{5,7},{6,4},{7,5},{8,10},{9,11},{10,... | collective-permute-start | bytes 1572872 | tf_op jit(solution)/shard_map/ppermute | solution.py:51
  9.2 79.7 %collective-permute-start.11 = (bf16[128,1024]{1,0:T(8,128)(2,1)}, bf16[128,1024]{1,0:T(8,128)(2,1)}, u32[]{:S(2)}, u32[]{:S(2)}) collective-permute-start(bf16[128,1024]{1,0:T(8,128)(2,1)} %param.39), channel_id=1, source_target_pairs={{0,16},{4,20},{8,24},{12,28},{16,0},{20,4},{24,8},{28,12},{1,17},{... | collective-permute-start | bytes 786440 | tf_op jit(solution)/shard_map/ppermute | solution.py:51
  11.8 86.0 %collective-permute-start.14 = (bf16[256,1024]{1,0:T(8,128)(2,1)}, bf16[256,1024]{1,0:T(8,128)(2,1)}, u32[]{:S(2)}, u32[]{:S(2)}) collective-permute-start(bf16[256,1024]{1,0:T(8,128)(2,1)} %param.45), channel_id=1, source_target_pairs={{0,2},{1,3},{2,0},{3,1},{4,6},{5,7},{6,4},{7,5},{8,10},{9,11},{10,... | collective-permute-start | bytes 1572872 | tf_op jit(solution)/shard_map/ppermute | solution.py:51
  22.2 10.6 %collective-permute-start.6 = (bf16[2,256,128]{2,1,0:T(8,128)(2,1)S(1)}, bf16[2,256,128]{2,1,0:T(8,128)(2,1)S(1)}, u32[]{:S(2)}, u32[]{:S(2)}) collective-permute-start(bf16[2,256,128]{2,1,0:T(8,128)(2,1)S(1)} %maximum_select_fusion.22), channel_id=1, source_target_pairs={{0,8},{4,12},{8,0},{12,4},{16,24},{20,28},{24,16},{28,20},{1,9},{5... | collective-permute-start | bytes 393224 | tf_op jit(solution)/shard_map/ppermute | solution.py:51
  32.9 14.9 %collective-permute-start.7 = (bf16[2,2,256,128]{3,2,1,0:T(8,128)(2,1)S(1)}, bf16[2,2,256,128]{3,2,1,0:T(8,128)(2,1)S(1)}, u32[]{:S(2)}, u32[]{:S(2)}) collective-permute-start(bf16[2,2,256,128]{3,2,1,0:T(8,128)(2,1)S(1)} %maximum_select_fusion.20), channel_id=1, source_target_pairs={{0,4},{4,0},{8,12},{12,8},{16,20},{20,16},{24,28},{28,24},{1,5},{5... | collective-permute-start | bytes 786440 | tf_op jit(solution)/shard_map/ppermute | solution.py:51
  34.6 10.8 %collective-permute-start.3 = (bf16[2,128,768]{2,1,0:T(8,128)(2,1)S(1)}, bf16[2,128,768]{2,1,0:T(8,128)(2,1)S(1)}, u32[]{:S(2)}, u32[]{:S(2)}) collective-permute-start(bf16[2,128,768]{2,1,0:T(8,128)(2,1)S(1)} %maximum_select_fusion.19), channel_id=1, source_target_pairs={{0,8},{4,12},{8,0},{12,4},{16,24},{20,28},{24,16},{28,20},{1,9},{5... | collective-permute-start | bytes 1179656 | tf_op jit(solution)/shard_map/ppermute | solution.py:51
  35.9 30.8 %collective-permute-start.1 = (bf16[2,256,1024]{2,1,0:T(8,128)(2,1)}, bf16[2,256,1024]{2,1,0:T(8,128)(2,1)S(1)}, u32[]{:S(2)}, u32[]{:S(2)}) collective-permute-start(bf16[2,256,1024]{2,1,0:T(8,128)(2,1)} %maximum_select_fusion.7), channel_id=1, source_target_pairs={{0,1},{1,0},{2,3},{3,2},{4,5},{5,4},{6,7},{7,6},{8,9},{9,8},{10,11... | collective-permute-start | bytes 3145736 | tf_op jit(solution)/shard_map/ppermute | solution.py:51
  46.4 18.6 %collective-permute-start.4 = (bf16[2,2,128,768]{3,2,1,0:T(8,128)(2,1)}, bf16[2,2,128,768]{3,2,1,0:T(8,128)(2,1)}, u32[]{:S(2)}, u32[]{:S(2)}) collective-permute-start(bf16[2,2,128,768]{3,2,1,0:T(8,128)(2,1)} %maximum_select_fusion.12), channel_id=1, source_target_pairs={{0,4},{4,0},{8,12},{12,8},{16,20},{20,16},{24,28},{28,24},{1,5},{5... | collective-permute-start | bytes 2359304 | tf_op jit(solution)/shard_map/ppermute | solution.py:51
  47.8 42.9 %collective-permute-start.16 = (bf16[1024,128]{1,0:T(8,128)(2,1)S(1)}, bf16[1024,128]{1,0:T(8,128)(2,1)}, u32[]{:S(2)}, u32[]{:S(2)}) collective-permute-start(bf16[1024,128]{1,0:T(8,128)(2,1)S(1)} %copy-done.25), channel_id=1, source_target_pairs={{0,16},{4,20},{8,24},{12,28},{16,0},{20,4},{24,8},{28,12},{1,17},{... | collective-permute-start | bytes 786440 | tf_op jit(solution)/shard_map/ppermute | solution.py:51
  88.8 17.7 %collective-permute-start.8 = (bf16[512,1024]{1,0:T(8,128)(2,1)S(1)}, bf16[512,1024]{1,0:T(8,128)(2,1)S(1)}, u32[]{:S(2)}, u32[]{:S(2)}) collective-permute-start(bf16[512,1024]{1,0:T(8,128)(2,1)S(1)} %convolution_convert_fusion.5), channel_id=1, source_target_pairs={{0,1},{1,0},{2,3},{3,2},{4,5},{5,4},{6,7},{7,6},{8,9},{9,8},{10,11... | collective-permute-start | bytes 3145736 | tf_op jit(solution)/shard_map/ppermute | solution.py:51
  90.1 14.9 %collective-permute-start.12 = (bf16[2,128,1024]{2,1,0:T(8,128)(2,1)S(1)}, bf16[2,128,1024]{2,1,0:T(8,128)(2,1)S(1)}, u32[]{:S(2)}, u32[]{:S(2)}) collective-permute-start(bf16[2,128,1024]{2,1,0:T(8,128)(2,1)S(1)} %maximum_select_fusion.15), channel_id=1, source_target_pairs={{0,8},{4,12},{8,0},{12,4},{16,24},{20,28},{24,16},{28,20},{1,9},{5... | collective-permute-start | bytes 1572872 | tf_op jit(solution)/shard_map/ppermute | solution.py:51
  91.8 23.9 %collective-permute-start.17 = (bf16[2,1024,128]{2,1,0:T(8,128)(2,1)S(1)}, bf16[2,1024,128]{2,1,0:T(8,128)(2,1)S(1)}, u32[]{:S(2)}, u32[]{:S(2)}) collective-permute-start(bf16[2,1024,128]{2,1,0:T(8,128)(2,1)S(1)} %maximum_select_fusion.17), channel_id=1, source_target_pairs={{0,8},{4,12},{8,0},{12,4},{16,24},{20,28},{24,16},{28,20},{1,9},{5... | collective-permute-start | bytes 1572872 | tf_op jit(solution)/shard_map/ppermute | solution.py:51
  99.2 37.1 %collective-permute-start.15 = (bf16[2,256,1024]{2,1,0:T(8,128)(2,1)S(1)}, bf16[2,256,1024]{2,1,0:T(8,128)(2,1)S(1)}, u32[]{:S(2)}, u32[]{:S(2)}) collective-permute-start(bf16[2,256,1024]{2,1,0:T(8,128)(2,1)S(1)} %maximum_select_fusion.10), channel_id=1, source_target_pairs={{0,1},{1,0},{2,3},{3,2},{4,5},{5,4},{6,7},{7,6},{8,9},{9,8},{10,11... | collective-permute-start | bytes 3145736 | tf_op jit(solution)/shard_map/ppermute | solution.py:51
  106.1 52.6 %collective-permute-start.13 = (bf16[2,2,128,1024]{3,2,1,0:T(8,128)(2,1)}, bf16[2,2,128,1024]{3,2,1,0:T(8,128)(2,1)}, u32[]{:S(2)}, u32[]{:S(2)}) collective-permute-start(bf16[2,2,128,1024]{3,2,1,0:T(8,128)(2,1)} %maximum_select_fusion.8), channel_id=1, source_target_pairs={{0,4},{4,0},{8,12},{12,8},{16,20},{20,16},{24,28},{28,24},{1,5},{5... | collective-permute-start | bytes 3145736 | tf_op jit(solution)/shard_map/ppermute | solution.py:51
  107.1 24.0 %collective-permute-start.9 = (bf16[512,1024]{1,0:T(8,128)(2,1)S(1)}, bf16[512,1024]{1,0:T(8,128)(2,1)S(1)}, u32[]{:S(2)}, u32[]{:S(2)}) collective-permute-start(bf16[512,1024]{1,0:T(8,128)(2,1)S(1)} %get-tuple-element.201), channel_id=1, source_target_pairs={{0,2},{1,3},{2,0},{3,1},{4,6},{5,7},{6,4},{7,5},{8,10},{9,11},{10,... | collective-permute-start | bytes 3145736 | tf_op jit(solution)/shard_map/ppermute | solution.py:51
  115.8 37.1 %collective-permute-start.18 = (bf16[2,2,1024,128]{3,2,1,0:T(8,128)(2,1)S(1)}, bf16[2,2,1024,128]{3,2,1,0:T(8,128)(2,1)S(1)}, u32[]{:S(2)}, u32[]{:S(2)}) collective-permute-start(bf16[2,2,1024,128]{3,2,1,0:T(8,128)(2,1)S(1)} %maximum_select_fusion.11), channel_id=1, source_target_pairs={{0,4},{4,0},{8,12},{12,8},{16,20},{20,16},{24,28},{28,24},{1,5},{5... | collective-permute-start | bytes 3145736 | tf_op jit(solution)/shard_map/ppermute | solution.py:51
  136.3 24.2 %collective-permute-start.10 = (bf16[2,256,1024]{2,1,0:T(8,128)(2,1)}, bf16[2,256,1024]{2,1,0:T(8,128)(2,1)}, u32[]{:S(2)}, u32[]{:S(2)}) collective-permute-start(bf16[2,256,1024]{2,1,0:T(8,128)(2,1)} %bitcast.35), channel_id=1, source_target_pairs={{0,1},{1,0},{2,3},{3,2},{4,5},{5,4},{6,7},{7,6},{8,9},{9,8},{10,11... | collective-permute-start | bytes 3145736 | tf_op jit(solution)/shard_map/ppermute | solution.py:51
  194.1 4.2 collective-permute-start.20
  207.9 26.3 %collective-permute-start.47 = (bf16[1024,512]{0,1:T(8,128)(2,1)}, bf16[1024,512]{0,1:T(8,128)(2,1)}, u32[]{:S(2)}, u32[]{:S(2)}) collective-permute-start(bf16[1024,512]{0,1:T(8,128)(2,1)} %convolution_convert_fusion.1), channel_id=1, source_target_pairs={{0,4},{4,0},{8,12},{12,8},{16,20},{20,16},{24,28},{28,24},{1,5},{5... | collective-permute-start | bytes 3145736 | tf_op jit(solution)/shard_map/ppermute | solution.py:51
  210.7 45.2 %collective-permute-start.44 = (bf16[512,1024]{1,0:T(8,128)(2,1)}, bf16[512,1024]{1,0:T(8,128)(2,1)}, u32[]{:S(2)}, u32[]{:S(2)}) collective-permute-start(bf16[512,1024]{1,0:T(8,128)(2,1)} %convolution_convert_fusion.2), channel_id=1, source_target_pairs={{0,4},{4,0},{8,12},{12,8},{16,20},{20,16},{24,28},{28,24},{1,5},{5... | collective-permute-start | bytes 3145736 | tf_op jit(solution)/shard_map/ppermute | solution.py:51
  216.1 44.0 %collective-permute-start.23 = (bf16[512,1024]{1,0:T(8,128)(2,1)}, bf16[512,1024]{1,0:T(8,128)(2,1)}, u32[]{:S(2)}, u32[]{:S(2)}) collective-permute-start(bf16[512,1024]{1,0:T(8,128)(2,1)} %convolution_convert_fusion.3), channel_id=1, source_target_pairs={{0,1},{1,0},{2,3},{3,2},{4,5},{5,4},{6,7},{7,6},{8,9},{9,8},{10,11... | collective-permute-start | bytes 3145736 | tf_op jit(solution)/shard_map/ppermute | solution.py:51
  220.2 42.9 %collective-permute-start.21 = (bf16[512,1024]{1,0:T(8,128)(2,1)S(1)}, bf16[512,1024]{1,0:T(8,128)(2,1)S(1)}, u32[]{:S(2)}, u32[]{:S(2)}) collective-permute-start(bf16[512,1024]{1,0:T(8,128)(2,1)S(1)} %convolution_convert_fusion.4), channel_id=1, source_target_pairs={{0,1},{1,0},{2,3},{3,2},{4,5},{5,4},{6,7},{7,6},{8,9},{9,8},{10,11... | collective-permute-start | bytes 3145736 | tf_op jit(solution)/shard_map/ppermute | solution.py:51
  237.1 31.0 %collective-permute-start.48 = (bf16[1024,256]{0,1:T(8,128)(2,1)S(1)}, bf16[1024,256]{0,1:T(8,128)(2,1)S(1)}, u32[]{:S(2)}, u32[]{:S(2)}) collective-permute-start(bf16[1024,256]{0,1:T(8,128)(2,1)S(1)} %pad_maximum_fusion.6), channel_id=1, source_target_pairs={{0,8},{4,12},{8,0},{12,4},{16,24},{20,28},{24,16},{28,20},{1,9},{5... | collective-permute-start | bytes 1572872 | tf_op jit(solution)/shard_map/ppermute | solution.py:51
  259.5 39.0 %collective-permute-start.45 = (bf16[256,1024]{1,0:T(8,128)(2,1)}, bf16[256,1024]{1,0:T(8,128)(2,1)}, u32[]{:S(2)}, u32[]{:S(2)}) collective-permute-start(bf16[256,1024]{1,0:T(8,128)(2,1)} %bitcast.126), channel_id=1, source_target_pairs={{0,8},{4,12},{8,0},{12,4},{16,24},{20,28},{24,16},{28,20},{1,9},{5... | collective-permute-start | bytes 1572872 | tf_op jit(solution)/shard_map/ppermute | solution.py:51
  262.6 26.1 %collective-permute-start.24 = (bf16[512,1024]{1,0:T(8,128)(2,1)S(1)}, bf16[512,1024]{1,0:T(8,128)(2,1)S(1)}, u32[]{:S(2)}, u32[]{:S(2)}) collective-permute-start(bf16[512,1024]{1,0:T(8,128)(2,1)S(1)} %get-tuple-element.205), channel_id=1, source_target_pairs={{0,2},{1,3},{2,0},{3,1},{4,6},{5,7},{6,4},{7,5},{8,10},{9,11},{10,... | collective-permute-start | bytes 3145736 | tf_op jit(solution)/shard_map/ppermute | solution.py:51
  265.5 40.4 %collective-permute-start.22 = (bf16[256,1024]{1,0:T(8,128)(2,1)}, bf16[256,1024]{1,0:T(8,128)(2,1)}, u32[]{:S(2)}, u32[]{:S(2)}) collective-permute-start(bf16[256,1024]{1,0:T(8,128)(2,1)} %fusion.101), channel_id=1, source_target_pairs={{0,2},{1,3},{2,0},{3,1},{4,6},{5,7},{6,4},{7,5},{8,10},{9,11},{10,... | collective-permute-start | bytes 1572872 | tf_op jit(solution)/shard_map/ppermute | solution.py:51
  269.2 42.4 %collective-permute-start.49 = (bf16[1024,128]{0,1:T(8,128)(2,1)}, bf16[1024,128]{0,1:T(8,128)(2,1)}, u32[]{:S(2)}, u32[]{:S(2)}) collective-permute-start(bf16[1024,128]{0,1:T(8,128)(2,1)} %dynamic-slice_convert_fusion.4), channel_id=1, source_target_pairs={{0,16},{4,20},{8,24},{12,28},{16,0},{20,4},{24,8},{28,12},{1,17},{... | collective-permute-start | bytes 786440 | tf_op jit(solution)/shard_map/ppermute | solution.py:51
  300.2 5.1 %collective-permute-start.40 = (f32[18,1024]{1,0:T(8,128)S(1)}, f32[18,1024]{1,0:T(8,128)S(1)}, u32[]{:S(2)}, u32[]{:S(2)}) collective-permute-start(f32[18,1024]{1,0:T(8,128)S(1)} %add.701), channel_id=1, source_target_pairs={{0,2},{1,3},{2,0},{3,1},{4,6},{5,7},{6,4},{7,5},{8,10},{9,11},{10,... | collective-permute-start | bytes 221192 | tf_op jit(solution)/shard_map/ppermute | solution.py:51
  300.8 17.1 %collective-permute-start.46 = (bf16[128,1024]{1,0:T(8,128)(2,1)S(1)}, bf16[128,1024]{1,0:T(8,128)(2,1)S(1)}, u32[]{:S(2)}, u32[]{:S(2)}) collective-permute-start(bf16[128,1024]{1,0:T(8,128)(2,1)S(1)} %fusion.103), channel_id=1, source_target_pairs={{0,16},{4,20},{8,24},{12,28},{16,0},{20,4},{24,8},{28,12},{1,17},{... | collective-permute-start | bytes 786440 | tf_op jit(solution)/shard_map/ppermute | solution.py:51
  302.7 24.6 %collective-permute-start.25 = (bf16[2,256,1024]{2,1,0:T(8,128)(2,1)S(1)}, bf16[2,256,1024]{2,1,0:T(8,128)(2,1)}, u32[]{:S(2)}, u32[]{:S(2)}) collective-permute-start(bf16[2,256,1024]{2,1,0:T(8,128)(2,1)S(1)} %bitcast.248), channel_id=1, source_target_pairs={{0,1},{1,0},{2,3},{3,2},{4,5},{5,4},{6,7},{7,6},{8,9},{9,8},{10,11... | collective-permute-start | bytes 3145736 | tf_op jit(solution)/shard_map/ppermute | solution.py:51
  305.3 4.7 %collective-permute-start.41 = (f32[18,1024]{1,0:T(8,128)S(1)}, f32[18,1024]{1,0:T(8,128)S(1)}, u32[]{:S(2)}, u32[]{:S(2)}) collective-permute-start(f32[18,1024]{1,0:T(8,128)S(1)} %add.702), channel_id=1, source_target_pairs={{0,4},{4,0},{8,12},{12,8},{16,20},{20,16},{24,28},{28,24},{1,5},{5... | collective-permute-start | bytes 221192 | tf_op jit(solution)/shard_map/ppermute | solution.py:51
  310.0 7.7 %collective-permute-start.42 = (f32[18,1024]{1,0:T(8,128)S(1)}, f32[18,1024]{1,0:T(8,128)S(1)}, u32[]{:S(2)}, u32[]{:S(2)}) collective-permute-start(f32[18,1024]{1,0:T(8,128)S(1)} %add.703), channel_id=1, source_target_pairs={{0,8},{4,12},{8,0},{12,4},{16,24},{20,28},{24,16},{28,20},{1,9},{5... | collective-permute-start | bytes 221192 | tf_op jit(solution)/shard_map/ppermute | solution.py:51
  317.8 7.0 %collective-permute-start.43 = (f32[18,1024]{1,0:T(8,128)S(1)}, f32[18,1024]{1,0:T(8,128)S(1)}, u32[]{:S(2)}, u32[]{:S(2)}) collective-permute-start(f32[18,1024]{1,0:T(8,128)S(1)} %add.704), channel_id=1, source_target_pairs={{0,16},{4,20},{8,24},{12,28},{16,0},{20,4},{24,8},{28,12},{1,17},{... | collective-permute-start | bytes 221192 | tf_op jit(solution)/shard_map/ppermute | solution.py:51
  333.6 27.3 %collective-permute-start.36 = (bf16[256,512]{1,0:T(8,128)(2,1)}, bf16[256,512]{1,0:T(8,128)(2,1)}, u32[]{:S(2)}, u32[]{:S(2)}) collective-permute-start(bf16[256,512]{1,0:T(8,128)(2,1)} %convolution_convert_fusion.7), channel_id=1, source_target_pairs={{0,4},{4,0},{8,12},{12,8},{16,20},{20,16},{24,28},{28,24},{1,5},{5... | collective-permute-start | bytes 786440 | tf_op jit(solution)/shard_map/ppermute | solution.py:51
  355.7 19.5 %collective-permute-start.33 = (bf16[512,768]{1,0:T(8,128)(2,1)}, bf16[512,768]{1,0:T(8,128)(2,1)}, u32[]{:S(2)}, u32[]{:S(2)}) collective-permute-start(bf16[512,768]{1,0:T(8,128)(2,1)} %convolution_convert_fusion.6), channel_id=1, source_target_pairs={{0,4},{4,0},{8,12},{12,8},{16,20},{20,16},{24,28},{28,24},{1,5},{5... | collective-permute-start | bytes 2359304 | tf_op jit(solution)/shard_map/ppermute | solution.py:51
  360.2 17.6 %collective-permute-start.26 = (bf16[512,1024]{1,0:T(8,128)(2,1)}, bf16[512,1024]{1,0:T(8,128)(2,1)}, u32[]{:S(2)}, u32[]{:S(2)}) collective-permute-start(bf16[512,1024]{1,0:T(8,128)(2,1)} %convolution_convert_fusion), channel_id=1, source_target_pairs={{0,1},{1,0},{2,3},{3,2},{4,5},{5,4},{6,7},{7,6},{8,9},{9,8},{10,11... | collective-permute-start | bytes 3145736 | tf_op jit(solution)/shard_map/ppermute | solution.py:51
  364.0 6.2 %collective-permute-start.37 = (bf16[256,256]{1,0:T(8,128)(2,1)}, bf16[256,256]{1,0:T(8,128)(2,1)}, u32[]{:S(2)}, u32[]{:S(2)}) collective-permute-start(bf16[256,256]{1,0:T(8,128)(2,1)} %pad_maximum_fusion.9), channel_id=1, source_target_pairs={{0,8},{4,12},{8,0},{12,4},{16,24},{20,28},{24,16},{28,20},{1,9},{5... | collective-permute-start | bytes 393224 | tf_op jit(solution)/shard_map/ppermute | solution.py:51
  371.1 9.1 %collective-permute-start.38 = (bf16[256,128]{1,0:T(8,128)(2,1)S(1)}, bf16[256,128]{1,0:T(8,128)(2,1)S(1)}, u32[]{:S(2)}, u32[]{:S(2)}) collective-permute-start(bf16[256,128]{1,0:T(8,128)(2,1)S(1)} %dynamic-slice_convert_fusion.9), channel_id=1, source_target_pairs={{0,16},{4,20},{8,24},{12,28},{16,0},{20,4},{24,8},{28,12},{1,17},{... | collective-permute-start | bytes 196616 | tf_op jit(solution)/shard_map/ppermute | solution.py:51
  377.7 10.0 %collective-permute-start.34 = (bf16[256,768]{1,0:T(8,128)(2,1)S(1)}, bf16[256,768]{1,0:T(8,128)(2,1)S(1)}, u32[]{:S(2)}, u32[]{:S(2)}) collective-permute-start(bf16[256,768]{1,0:T(8,128)(2,1)S(1)} %bitcast.313), channel_id=1, source_target_pairs={{0,8},{4,12},{8,0},{12,4},{16,24},{20,28},{24,16},{28,20},{1,9},{5... | collective-permute-start | bytes 1179656 | tf_op jit(solution)/shard_map/ppermute | solution.py:51
  380.2 12.8 %collective-permute-start.27 = (bf16[256,1024]{1,0:T(8,128)(2,1)S(1)}, bf16[256,1024]{1,0:T(8,128)(2,1)S(1)}, u32[]{:S(2)}, u32[]{:S(2)}) collective-permute-start(bf16[256,1024]{1,0:T(8,128)(2,1)S(1)} %fusion.102), channel_id=1, source_target_pairs={{0,2},{1,3},{2,0},{3,1},{4,6},{5,7},{6,4},{7,5},{8,10},{9,11},{10,... | collective-permute-start | bytes 1572872 | tf_op jit(solution)/shard_map/ppermute | solution.py:51
  388.5 10.3 %collective-permute-start.35 = (bf16[128,768]{1,0:T(8,128)(2,1)}, bf16[128,768]{1,0:T(8,128)(2,1)}, u32[]{:S(2)}, u32[]{:S(2)}) collective-permute-start(bf16[128,768]{1,0:T(8,128)(2,1)} %fusion.104), channel_id=1, source_target_pairs={{0,16},{4,20},{8,24},{12,28},{16,0},{20,4},{24,8},{28,12},{1,17},{... | collective-permute-start | bytes 589832 | tf_op jit(solution)/shard_map/ppermute | solution.py:51
  394.6 5.2 %collective-permute-start.28 = (f32[5,1024]{1,0:T(8,128)S(1)}, f32[5,1024]{1,0:T(8,128)S(1)}, u32[]{:S(2)}, u32[]{:S(2)}) collective-permute-start(f32[5,1024]{1,0:T(8,128)S(1)} %concatenate.264), channel_id=1, source_target_pairs={{0,1},{1,0},{2,3},{3,2},{4,5},{5,4},{6,7},{7,6},{8,9},{9,8},{10,11... | collective-permute-start | bytes 61448 | tf_op jit(solution)/shard_map/ppermute | solution.py:51
  399.8 4.0 collective-permute-start.29
  403.7 3.9 collective-permute-start.30
  407.7 4.3 %collective-permute-start.31 = (f32[5,1024]{1,0:T(8,128)S(1)}, f32[5,1024]{1,0:T(8,128)S(1)}, u32[]{:S(2)}, u32[]{:S(2)}) collective-permute-start(f32[5,1024]{1,0:T(8,128)S(1)} %add.666), channel_id=1, source_target_pairs={{0,8},{4,12},{8,0},{12,4},{16,24},{20,28},{24,16},{28,20},{1,9},{5... | collective-permute-start | bytes 61448 | tf_op jit(solution)/shard_map/ppermute | solution.py:51
  411.9 4.8 %collective-permute-start.32 = (f32[5,1024]{1,0:T(8,128)S(1)}, f32[5,1024]{1,0:T(8,128)S(1)}, u32[]{:S(2)}, u32[]{:S(2)}) collective-permute-start(f32[5,1024]{1,0:T(8,128)S(1)} %add.667), channel_id=1, source_target_pairs={{0,16},{4,20},{8,24},{12,28},{16,0},{20,4},{24,8},{28,12},{1,17},{... | collective-permute-start | bytes 61448 | tf_op jit(solution)/shard_map/ppermute | solution.py:51
  (80 other events, 736.5 us)
